TPU v7x, 32 devices: a whole 2x2x4 slice. The times are simulated.
32 devices in a mesh: grp: 2 (over x), seq: 4 (over y, core), tp: 4 (over z).
Axes of the slice: x: 2, y: 2, z: 4, core: 2. Of those that a mesh axis runs over, the one named last changes fastest.
Arguments:
- prompt: bfloat16 [2048, 5376], P(('grp', 'seq'), 'tp'), parts along dimension 0, may hold values from -8 to 8, as said below
- cont_ids: int32 [16, 64], P('grp'), parts along dimension 0, may hold values from 0 to 131071
- embed: bfloat16 [131072, 5376], P('seq', 'tp'), may hold values from -0.078125 to 0.078125
- pre_gain: float32 [5376], replicated, may hold values from 0.5 to 1.5
- w_query: bfloat16 [5376, 4096], P('seq', 'tp'), may hold values from -0.078125 to 0.078125
- w_keyval: bfloat16 [5376, 2, 2048], P('seq', None, 'tp'), may hold values from -0.078125 to 0.078125
- q_gain: float32 [128], replicated, may hold values from 0.25 to 1.75
- k_gain: float32 [128], replicated, may hold values from 0.25 to 1.75
- w_out: bfloat16 [4096, 5376], P('tp', 'seq'), may hold values from -0.09375 to 0.09375
- post_gain: float32 [5376], replicated, may hold values from 0.5 to 1.5
Outputs:
- prompt_out: bfloat16 [2048, 5376], P(('grp', 'seq'), 'tp'), parts along dimension 0
- cont_out: bfloat16 [16, 64, 5376], P(('grp', 'seq'), None, 'tp'), parts along dimension 0
There are 2 independent parts, one for each index of `grp`. A program takes and returns all parts, laid end to end along the dimension named above; an argument that names none is the same for every part. Nothing has to cross between parts.
Inputs may be any that keep to these rules, and one draw needn't show every extreme that they name: `prompt`: values are rough from entry to entry.
All inputs are finite; a program needn't handle non-finite values.
Results may differ from a plain program's by a relative error of at most 0.014.
Values may be sent and summed in bfloat16 or wider, within the bound.
No kernel may reach another device: no remote copies, remote signals or barrier semaphores. Data moves between devices by JAX's collectives and lax.ppermute only.
A program may use at most 256 MiB of HBM per device.

v0:
```python
import math

import jax
import jax.numpy as jnp
from jax import lax
from jax.sharding import PartitionSpec as P

WINDOW = 1024


eps_norm = 1e-06
query_scalar = 168.0
rope_base = 10000.0


def from_behind(value, axis, by):
    count = lax.axis_size(axis)
    pairs = [(i, i + by) for i in range(count) if 0 <= i + by < count]
    return lax.ppermute(value, axis, pairs)


def from_root(value, axis, root):
    mine = lax.axis_index(axis) == root
    return lax.psum(jnp.where(mine, value, jnp.zeros_like(value)), axis)


def rms_scale(values, gain):
    mean_sq = jnp.mean(values * values, axis=-1, keepdims=True)
    return values * lax.rsqrt(mean_sq + eps_norm) * gain


def rotate(values, positions):
    half = values.shape[-1] // 2
    freqs = rope_base ** (
        -(jnp.arange(half, dtype=jnp.int32).astype(jnp.float32) * 2.0) / values.shape[-1]
    )
    angles = positions.astype(jnp.float32)[:, None] * freqs[None, :]
    cosine = jnp.cos(angles)[:, None, :]
    sine = jnp.sin(angles)[:, None, :]
    first = values[..., :half]
    second = values[..., half:]
    return jnp.concatenate(
        [first * cosine - second * sine, second * cosine + first * sine], axis=-1
    )


def attend(queries, keys, values, allowed):
    rows, heads, width = queries.shape
    kv_heads = keys.shape[1]
    grouped = queries.reshape(rows, kv_heads, heads // kv_heads, width)
    scores = jnp.einsum(
        "qkgd,nkd->kgqn", grouped, keys, preferred_element_type=jnp.float32
    ) * query_scalar ** (-0.5)
    scores = jnp.where(allowed[None, None], scores, -1e30)
    top = jnp.max(scores, axis=-1, keepdims=True)
    weights = jnp.exp(scores - top)
    weights = (weights / jnp.sum(weights, axis=-1, keepdims=True)).astype(jnp.bfloat16)
    mixed = jnp.einsum("kgqn,nkd->qkgd", weights, values, preferred_element_type=jnp.float32)
    return mixed.reshape(rows, heads * width).astype(jnp.bfloat16)


def on_device(
    prompt, cont_ids, embed, pre_gain, w_query, w_keyval, q_gain, k_gain, w_out, post_gain
):
    tok_rows, local_cols = prompt.shape
    n_seq = lax.axis_size("seq")
    n_tp = lax.axis_size("tp")
    seq_index = lax.axis_index("seq")
    tp_index = lax.axis_index("tp")
    full_width = local_cols * n_tp
    cont_count, cont_len = cont_ids.shape
    own_conts = cont_count // n_seq
    cont_rows = own_conts * cont_len
    vocab_rows = embed.shape[0]
    flat_ids = cont_ids.reshape(-1)
    vocab_start = seq_index * vocab_rows
    chosen = flat_ids - vocab_start
    inside = (chosen >= 0) & (chosen < vocab_rows)
    picked = jnp.take(embed, jnp.clip(chosen, 0, vocab_rows - 1), axis=0)
    embedded = lax.psum_scatter(
        jnp.where(inside[:, None], picked.astype(jnp.float32), 0.0).astype(jnp.bfloat16),
        "seq",
        scatter_dimension=0,
        tiled=True,
    ).astype(jnp.float32)
    cont_x = (embedded * math.sqrt(full_width)).astype(jnp.bfloat16)
    rows_x = jnp.concatenate([prompt, cont_x], axis=0)
    whole = lax.all_gather(rows_x, "tp", axis=1, tiled=True)
    normed = rms_scale(whole.astype(jnp.float32), pre_gain).astype(jnp.bfloat16)
    all_rows = normed.shape[0]
    q_cols = w_query.shape[1]
    kv_cols = w_keyval.shape[2]
    query_part = jnp.dot(
        normed,
        lax.all_gather(w_query, "seq", axis=0, tiled=True),
        preferred_element_type=jnp.float32,
    )
    kv_part = jnp.einsum(
        "rd,dcf->rcf",
        normed,
        lax.all_gather(w_keyval, "seq", axis=0, tiled=True),
        preferred_element_type=jnp.float32,
    )
    head_dim = q_gain.shape[0]
    q_heads = q_cols // head_dim
    kv_heads = kv_cols // head_dim
    tokens_total = n_seq * tok_rows
    positions = jnp.concatenate(
        [
            seq_index * tok_rows + jnp.arange(tok_rows, dtype=jnp.int32),
            tokens_total + jnp.arange(cont_rows, dtype=jnp.int32) % cont_len,
        ]
    )
    queries = rotate(
        rms_scale(query_part.reshape(all_rows, q_heads, head_dim), q_gain), positions
    ).astype(jnp.bfloat16)
    keys = rotate(
        rms_scale(kv_part[:, 0].reshape(all_rows, kv_heads, head_dim), k_gain), positions
    ).astype(jnp.bfloat16)
    values = kv_part[:, 1].astype(jnp.bfloat16)
    keyval = jnp.stack([keys.reshape(all_rows, kv_cols), values], axis=1)
    prompt_kv = keyval[:tok_rows]
    cont_kv = keyval[tok_rows:]
    reach = WINDOW // tok_rows
    earlier = []
    moving = prompt_kv
    for step in range(reach):
        moving = from_behind(moving, "seq", 1)
        earlier = [moving] + earlier
    band = jnp.concatenate(earlier + [prompt_kv], axis=0)
    q_pos = positions[:tok_rows]
    key_pos = seq_index * tok_rows - reach * tok_rows + jnp.arange(band.shape[0], dtype=jnp.int32)
    allowed = (
        (key_pos[None, :] <= q_pos[:, None])
        & (key_pos[None, :] > q_pos[:, None] - WINDOW)
        & (key_pos[None, :] >= 0)
    )
    prompt_mix = attend(
        queries[:tok_rows],
        band[:, 0].reshape(-1, kv_heads, head_dim),
        band[:, 1].reshape(-1, kv_heads, head_dim),
        allowed,
    )
    final = from_root(band[band.shape[0] - WINDOW :], "seq", n_seq - 1)
    spots = jnp.arange(cont_len, dtype=jnp.int32)
    allowed_cont = jnp.concatenate(
        [
            jnp.arange(WINDOW, dtype=jnp.int32)[None, :] > spots[:, None],
            spots[None, :] <= spots[:, None],
        ],
        axis=1,
    )
    cont_q = queries[tok_rows:].reshape(own_conts, cont_len, q_heads, head_dim)
    cont_keys = cont_kv.reshape(own_conts, cont_len, 2, kv_cols)

    def one_cont(query_block, key_block):
        joined = jnp.concatenate([final, key_block], axis=0)
        return attend(
            query_block,
            joined[:, 0].reshape(-1, kv_heads, head_dim),
            joined[:, 1].reshape(-1, kv_heads, head_dim),
            allowed_cont,
        )

    cont_mix = jax.vmap(one_cont)(cont_q, cont_keys).reshape(cont_rows, q_cols)
    mixed = jnp.concatenate([prompt_mix, cont_mix], axis=0)
    partial_rows = jnp.dot(
        mixed, lax.all_gather(w_out, "seq", axis=1, tiled=True), preferred_element_type=jnp.float32
    )
    attn_proj = lax.psum_scatter(
        partial_rows.astype(jnp.bfloat16), "tp", scatter_dimension=1, tiled=True
    ).astype(jnp.float32)
    row_sq = lax.psum(jnp.sum(attn_proj * attn_proj, axis=1), "tp")
    factor = lax.rsqrt(row_sq / full_width + eps_norm)
    gain_part = lax.dynamic_slice_in_dim(post_gain, tp_index * local_cols, local_cols)
    result = (rows_x.astype(jnp.float32) + attn_proj * factor[:, None] * gain_part).astype(
        jnp.bfloat16
    )
    return (result[:tok_rows], result[tok_rows:].reshape(own_conts, cont_len, local_cols))


def solution(mesh):
    return jax.shard_map(
        on_device,
        mesh=mesh,
        in_specs=(
            P(("grp", "seq"), "tp"),
            P("grp", None),
            P("seq", "tp"),
            P(),
            P("seq", "tp"),
            P("seq", None, "tp"),
            P(),
            P(),
            P("tp", "seq"),
            P(),
        ),
        out_specs=(P(("grp", "seq"), "tp"), P(("grp", "seq"), None, "tp")),
        check_vma=False,
    )
```

profile of v0, /device:TPU:0, one launch (start us, length us, event | category | flops | bytes accessed | tf_op | source)
XLA Modules:
  0.0 654.4 jit_solution(15897168828762125381)
XLA Ops:
  7.2 0.7 subtract_clamp_fusion
  8.1 0.7 compare_and_fusion
  8.8 106.7 %copy.74 = bf16[32768,1344]{1,0:T(8,128)(2,1)} copy(bf16[32768,1344]{0,1:T(8,128)(2,1)} %param.12) | data formatting | bytes 176160768 | tf_op args[2]
  115.5 16.8 %gather_fusion = bf16[512,1344]{1,0:T(8,128)(2,1)S(1)} fusion(bf16[32768,1344]{1,0:T(8,128)(2,1)} %copy.74, s32[1024]{0:T(1024)S(1)} %pad_clamp_fusion), kind=kCustom, calls=%fused_computation | custom fusion | bytes 2754560 | tf_op jit(solution)/shard_map/jit(_take)/gather | solution.py:79
  132.3 0.7 copy.75
  133.4 1.5 copy.108
  135.0 29.8 %reduce-scatter.7.cloned.1.call-done = bf16[128,1344]{1,0:T(8,128)(2,1)} async-done(((bf16[512,1344]{1,0:T(8,128)(2,1)}), bf16[128,1344]{1,0:T(8,128)(2,1)}) %reduce-scatter.7.cloned.1.call-update) | async-done | bytes 344080
  164.8 1.2 copy.109
  166.1 2.2 pad_maximum_fusion.1
  168.4 1.9 copy.76
  170.4 0.5 all-gather.9.cloned.1.call-update
  170.9 0.6 all-reduce.2.cloned.1.call-start
  171.5 0.8 multiply_cosine_fusion
  172.3 75.8 %all-gather.5.cloned.1.call-done = bf16[384,5376]{0,1:T(8,128)(2,1)} async-done(((bf16[384,1344]{0,1:T(8,128)(2,1)}), bf16[384,5376]{0,1:T(8,128)(2,1)}) %all-gather.5.cloned.1.call-update) | async-done | bytes 4128784 | tf_op jit(solution)/shard_map/all_gather | solution.py:88
  248.1 3.1 fusion.3
  251.3 70.1 %all-gather.7.cloned.1.call-done = bf16[5376,2,512]{2,0,1:T(8,128)(2,1)} async-done(((bf16[1344,2,512]{2,0,1:T(8,128)(2,1)}), bf16[5376,2,512]{2,0,1:T(8,128)(2,1)}) %all-gather.7.cloned.1.call-update) | async-done | bytes 11010064 | tf_op jit(solution)/shard_map/all_gather | solution.py:101
  321.4 9.9 %fusion.12 = f32[384,2,512]{2,0,1:T(8,128)S(1)} fusion(bf16[5376,2,512]{2,0,1:T(8,128)(2,1)} %all-gather.7.cloned.1.call-done, bf16[384,5376]{0,1:T(8,128)(2,1)} %all-gather.5.cloned.1.call-done, f32[5376]{0:T(1024)S(1)} %copy-done.16, f32[384]{0:T(512)S(1)} %add_rsqrt_fusion.3), kind=kOutput, calls=%fused_computation.25 | convolution fusion | flops 4236115968 | bytes 16734720 | tf_op jit(solution)/shard_map/rd,dcf->rcf/dot_general | solution.py:98
  331.7 0.5 multiply_reduce_fusion.1
  332.2 0.5 multiply_multiply_fusion
  332.7 0.7 subtract_convert_fusion.1
  333.4 0.5 pad_maximum_fusion.2
  334.2 2.2 collective-permute-start
  336.4 2.2 collective-permute-done
  338.6 17.3 %collective-permute-start.1 = (bf16[256,2,512]{2,0,1:T(8,128)(2,1)S(1)}, bf16[256,2,512]{2,0,1:T(8,128)(2,1)S(1)}, u32[]{:S(2)}, u32[]{:S(2)}) collective-permute-start(bf16[256,2,512]{2,0,1:T(8,128)(2,1)S(1)} %collective-permute-done), channel_id=1, source_target_pairs={{0,4},{4,8},{8,12},{1,5},{5,9},{9,13},{2,6},{6,10},{10,14},{3,7},{... | collective-permute-start | bytes 1572872 | tf_op jit(solution)/shard_map/ppermute | solution.py:19
  355.9 1.5 collective-permute-done.1
  357.4 20.4 %collective-permute-start.2 = (bf16[256,2,512]{2,0,1:T(8,128)(2,1)S(1)}, bf16[256,2,512]{2,0,1:T(8,128)(2,1)S(1)}, u32[]{:S(2)}, u32[]{:S(2)}) collective-permute-start(bf16[256,2,512]{2,0,1:T(8,128)(2,1)S(1)} %collective-permute-done.1), channel_id=1, source_target_pairs={{0,4},{4,8},{8,12},{1,5},{5,9},{9,13},{2,6},{6,10},{10,14},{3,7},{... | collective-permute-start | bytes 1572872 | tf_op jit(solution)/shard_map/ppermute | solution.py:19
  377.8 1.5 collective-permute-done.2
  379.3 1.8 maximum_select_fusion
  381.2 0.5 all-gather.11.cloned.1.call-update
  382.0 0.6 pad_add_fusion
  382.6 1.6 and_and_fusion
  384.2 24.7 %all-gather.9.cloned.1.call-done = bf16[5376,1024]{1,0:T(8,128)(2,1)} async-done(((bf16[1344,1024]{1,0:T(8,128)(2,1)}), bf16[5376,1024]{1,0:T(8,128)(2,1)}) %all-gather.9.cloned.1.call-update) | async-done | bytes 11010064 | tf_op jit(solution)/shard_map/all_gather | solution.py:95
  408.9 9.9 %fusion.27 = f32[384,1024]{1,0:T(8,128)S(1)} fusion(bf16[5376,1024]{1,0:T(8,128)(2,1)} %all-gather.9.cloned.1.call-done, bf16[384,5376]{0,1:T(8,128)(2,1)} %all-gather.5.cloned.1.call-done, f32[5376]{0:T(1024)S(1)} %copy-done.16, f32[384]{0:T(512)S(1)} %add_rsqrt_fusion.3), kind=kOutput, calls=%fused_computation.50 | convolution fusion | flops 4236115968 | bytes 16734720 | tf_op jit(solution)/shard_map/dot_general | solution.py:93
  419.2 1.2 multiply_reduce_fusion
  420.3 1.0 copy.80
  421.3 0.8 pad_maximum_fusion.4
  422.1 2.0 copy.86
  424.1 0.5 fusion.22
  424.6 0.5 copy-done.5
  425.1 2.1 collective-permute-start.3
  427.2 0.6 subtract_convert_fusion
  427.8 0.9 pad_maximum_fusion.3
  428.7 1.1 fusion.38
  430.2 1.3 reshape_squeeze.11
  431.5 1.4 copy.100
  433.0 4.8 fusion.65
  437.8 6.8 %fusion.25 = bf16[4,128,2,256]{3,1,2,0:T(8,128)(2,1)} fusion(bf16[1280,4,128,1]{0,2,3,1:T(8,128)(2,1)S(1)} %bitcast.77, f32[4,2,256]{2,1,0:T(2,128)S(1)} %fusion.65, pred[256,1280]{0,1:T(8,128)(4,1)} %and_and_fusion, bf16[256,4,2,128]{3,0,2,1:T(8,128)(2,1)S(1)} %bitcast.80, bf16[1280,4,128,1]{2,1,0,3:T(4,128)(2,1)S(1)} %bitcast.76), kind=kOutput, calls=%fused_computation.48 | convolution fusion | flops 1355549952 | bytes 4005888 | tf_op jit(solution)/shard_map/kgqn,nkd->qkgd/dot_general | solution.py:58
  444.6 24.6 %all-reduce.2.cloned.1.call-done = bf16[1024,2,512]{2,0,1:T(8,128)(2,1)} async-done(((bf16[1024,2,512]{2,0,1:T(8,128)(2,1)}), bf16[1024,2,512]{2,0,1:T(8,128)(2,1)}) %all-reduce.2.cloned.1.call-update) | async-done | bytes 2097168 | tf_op jit(solution)/shard_map/psum | solution.py:24
  469.2 3.0 copy.85
  472.2 0.5 broadcast_in_dim.53
  472.7 0.5 copy-done.6
  473.3 1.9 pad_maximum_fusion
  475.1 6.0 exponential_reduce_fusion
  481.2 4.4 fusion.30
  485.5 0.4 copy.107
  486.2 57.7 %all-gather.11.cloned.1.call-done = bf16[1024,5376]{0,1:T(8,128)(2,1)} async-done(((bf16[1024,1344]{0,1:T(8,128)(2,1)}), bf16[1024,5376]{0,1:T(8,128)(2,1)}) %all-gather.11.cloned.1.call-update) | async-done | bytes 11010064 | tf_op jit(solution)/shard_map/all_gather | solution.py:168
  543.9 11.5 %convolution_convert_fusion = bf16[384,5376]{0,1:T(8,128)(2,1)} fusion(bf16[1024,5376]{0,1:T(8,128)(2,1)} %all-gather.11.cloned.1.call-done, bf16[128,1024]{0,1:T(8,128)(2,1)S(1)} %reshape.287, bf16[256,1024]{0,1:T(8,128)(2,1)S(1)} %bitcast.84), kind=kOutput, calls=%fused_computation.9 | convolution fusion | flops 4231495680 | bytes 15925248 | tf_op jit(solution)/shard_map/dot_general | solution.py:167
  555.4 0.8 dynamic_slice.3
  556.3 75.0 %reduce-scatter.5.cloned.1.call-done = bf16[384,1344]{0,1:T(8,128)(2,1)} async-done(((bf16[384,5376]{0,1:T(8,128)(2,1)}), bf16[384,1344]{0,1:T(8,128)(2,1)}) %reduce-scatter.5.cloned.1.call-update) | async-done | bytes 1032208 | tf_op jit(solution)/shard_map/reduce_scatter | solution.py:170
  631.3 1.5 fusion.18
  632.8 11.0 %psum.15 = f32[384]{0:T(512)S(1)} all-reduce(f32[384]{0:T(512)S(1)} %fusion.18), channel_id=1, replica_groups=mesh['grp'=2,'seq'=4,'tp'=4] {'tp'}, use_global_device_ids=true, to_apply=%region_11.12 | all-reduce | flops 384 | bytes 3072 | tf_op jit(solution)/shard_map/psum | solution.py:173
  643.8 1.6 fusion.21
  645.5 0.9 slice.83
  646.4 0.9 copy.92
  (81 shorter events, 3.0 us)
Async XLA Ops:
  7.2 157.6 %reduce-scatter.7.cloned.1.call-start = ((), (), s32[]{:S(2)}) async-start(), calls=%async_computation.8 | async-start | bytes 1802240
  134.9 33.4 %copy-start = (bf16[1344,2,512]{2,1,0:T(2,128)(2,1)S(1)}, bf16[1344,2,512]{2,1,0:T(2,128)(2,1)}, u32[]{:S(2)}) copy-start(bf16[1344,2,512]{2,1,0:T(2,128)(2,1)} %param.15) | copy-start | bytes 8257540
  135.0 113.1 %all-gather.5.cloned.1.call-start = ((), (), s32[]{:S(2)}) async-start(), calls=%async_computation.2 | async-start | bytes 5160960 | tf_op jit(solution)/shard_map/all_gather | solution.py:88
  168.3 153.1 %all-gather.7.cloned.1.call-start = ((), (), s32[]{:S(2)}) async-start(), calls=%async_computation.3 | async-start | bytes 13762560 | tf_op jit(solution)/shard_map/all_gather | solution.py:101
  170.3 238.6 %all-gather.9.cloned.1.call-start = ((), (), s32[]{:S(2)}) async-start(), calls=%async_computation.4 | async-start | bytes 13762560 | tf_op jit(solution)/shard_map/all_gather | solution.py:95
  170.9 150.5 %copy-start.16 = (f32[5376]{0:T(1024)S(1)}, f32[5376]{0:T(1024)}, u32[]{:S(2)}) copy-start(f32[5376]{0:T(1024)} %param.13) | copy-start | bytes 64516
  170.9 298.3 %all-reduce.2.cloned.1.call-start = ((), (), s32[]{:S(2)}) async-start(), calls=%async_computation.5 | async-start | bytes 4194304 | tf_op jit(solution)/shard_map/psum | solution.py:24
  172.3 160.4 %copy-start.7 = (f32[384,64]{1,0:T(8,128)}, f32[384,64]{1,0:T(8,128)S(1)}, u32[]{:S(2)}) copy-start(f32[384,64]{1,0:T(8,128)S(1)} %get-tuple-element.13) | copy-start | bytes 294916
  331.3 0.9 copy-start.14
  334.2 4.4 collective-permute-start
  338.6 18.8 %collective-permute-start.1 = (bf16[256,2,512]{2,0,1:T(8,128)(2,1)S(1)}, bf16[256,2,512]{2,0,1:T(8,128)(2,1)S(1)}, u32[]{:S(2)}, u32[]{:S(2)}) collective-permute-start(bf16[256,2,512]{2,0,1:T(8,128)(2,1)S(1)} %collective-permute-done), channel_id=1, source_target_pairs={{0,4},{4,8},{8,12},{1,5},{5,9},{9,13},{2,6},{6,10},{10,14},{3,7},{... | collective-permute-start | bytes 1572872 | tf_op jit(solution)/shard_map/ppermute | solution.py:19
  357.4 23.7 %copy-start.2 = (bf16[256,2,512]{2,0,1:T(8,128)(2,1)}, bf16[256,2,512]{2,0,1:T(8,128)(2,1)S(1)}, u32[]{:S(2)}) copy-start(bf16[256,2,512]{2,0,1:T(8,128)(2,1)S(1)} %collective-permute-done.1) | copy-start | bytes 1572868
  357.4 21.8 %collective-permute-start.2 = (bf16[256,2,512]{2,0,1:T(8,128)(2,1)S(1)}, bf16[256,2,512]{2,0,1:T(8,128)(2,1)S(1)}, u32[]{:S(2)}, u32[]{:S(2)}) collective-permute-start(bf16[256,2,512]{2,0,1:T(8,128)(2,1)S(1)} %collective-permute-done.1), channel_id=1, source_target_pairs={{0,4},{4,8},{8,12},{1,5},{5,9},{9,13},{2,6},{6,10},{10,14},{3,7},{... | collective-permute-start | bytes 1572872 | tf_op jit(solution)/shard_map/ppermute | solution.py:19
  379.3 1.8 copy-start.4
  381.1 162.8 %all-gather.11.cloned.1.call-start = ((), (), s32[]{:S(2)}) async-start(), calls=%async_computation.6 | async-start | bytes 13762560 | tf_op jit(solution)/shard_map/all_gather | solution.py:168
  381.7 249.6 %reduce-scatter.5.cloned.1.call-start = ((), (), s32[]{:S(2)}) async-start(), calls=%async_computation.7 | async-start | bytes 5160960 | tf_op jit(solution)/shard_map/reduce_scatter | solution.py:170
  419.2 4.9 copy-start.15
  424.1 1.0 copy-start.5
  424.1 3.1 copy-start.8
  425.1 4.7 collective-permute-start.3
  427.8 2.1 copy-start.3
  430.2 2.8 copy-start.11
  431.5 1.5 copy-start.9
  433.0 4.8 copy-start.10
  472.2 1.0 copy-start.6
  473.2 1.9 copy-start.12
  473.3 1.9 copy-start.13
  481.2 62.7 %copy-start.17 = (bf16[4,128,2,256]{3,1,2,0:T(8,128)(2,1)S(1)}, bf16[4,128,2,256]{3,1,2,0:T(8,128)(2,1)}, u32[]{:S(2)}) copy-start(bf16[4,128,2,256]{3,1,2,0:T(8,128)(2,1)} %fusion.25) | copy-start | bytes 1572868
  555.4 88.4 %copy-start.1 = (bf16[256,1344]{0,1:T(8,128)(2,1)S(1)}, bf16[256,1344]{0,1:T(8,128)(2,1)}, u32[]{:S(2)}) copy-start(bf16[256,1344]{0,1:T(8,128)(2,1)} %param.10) | copy-start | bytes 2064388
Sparse Core Ops, SparseCore 0:
  135.1 29.6 reduce-scatter.6
  168.4 79.6 all-gather.4
  249.7 71.6 all-gather.6
  322.8 86.0 all-gather.8
  411.1 58.0 all-reduce.1
  470.6 73.2 all-gather.10
  555.6 75.7 reduce-scatter.4
where the time goes:
time: 662 us; the launch traced here: 654 us
  waiting for transfers between devices  364 us (55%)
  local copies, waits for them, and re-layouts  144 us (22%)
  matrix products  53.3 us (8%)
  starting transfers between devices  42.9 us (6%)
  other arithmetic  24.2 us (4%)
  between operations  14.9 us (2%)
  blocking collectives  11 us (2%)
    unnamed x45, local copies, waits for them, and re-layouts  113 us
    all_gather x1, waiting for transfers between devices, on_device(): whole = lax.all_gather(rows_x, 'tp', axis=1, tiled=True)  75.8 us
    reduce_scatter x1, waiting for transfers between devices, on_device(): lax.psum_scatter(partial_rows.astype(jnp.bfloat16), 'tp', scatter_dimensi...  75 us
    all_gather x1, waiting for transfers between devices, on_device(): lax.all_gather(w_keyval, 'seq', axis=0, tiled=True)  70.1 us
    all_gather x1, waiting for transfers between devices, on_device(): lax.all_gather(w_out, 'seq', axis=1, tiled=True)  57.7 us
    ppermute x4, starting transfers between devices, from_behind(): return lax.ppermute(value, axis, pairs)  41.9 us
    unnamed x8, waiting for transfers between devices  30.9 us
    all_gather x1, waiting for transfers between devices, on_device(): lax.all_gather(w_query, 'seq', axis=0, tiled=True)  24.7 us
  transfers between devices with their start and end apart: 11, of which 10 were waited for; matrix products, arithmetic and copies ran while one was open for 11% of the time, Pallas kernels for 0%

commit v1 on v0

--- a/solution.py
+++ b/solution.py
@@ -1,9 +1,13 @@
+import functools
 import math
 
 import jax
 import jax.numpy as jnp
 from jax import lax
+from jax.experimental import pallas as pl
+from jax.experimental.pallas import tpu as pltpu
 from jax.sharding import PartitionSpec as P
+
 
 WINDOW = 1024
 
@@ -59,7 +63,7 @@
     return mixed.reshape(rows, heads * width).astype(jnp.bfloat16)
 
 
-def on_device(
+def plain_device(
     prompt, cont_ids, embed, pre_gain, w_query, w_keyval, q_gain, k_gain, w_out, post_gain
 ):
     tok_rows, local_cols = prompt.shape
@@ -124,7 +128,7 @@
     reach = WINDOW // tok_rows
     earlier = []
     moving = prompt_kv
-    for step in range(reach):
+    for _ in range(reach):
         moving = from_behind(moving, "seq", 1)
         earlier = [moving] + earlier
     band = jnp.concatenate(earlier + [prompt_kv], axis=0)
@@ -179,9 +183,540 @@
     return (result[:tok_rows], result[tok_rows:].reshape(own_conts, cont_len, local_cols))
 
 
+ANY = pl.BlockSpec(memory_space=pl.ANY)
+SMEM = pl.BlockSpec(memory_space=pltpu.SMEM)
+VMEM = pl.BlockSpec(memory_space=pltpu.VMEM)
+BATCH = 8
+
+
+def pick_kernel(info, emb, lanes, listed, ids, out, buf, held, acc, sems):
+    rounds = (info[0] + BATCH - 1) // BATCH
+    width = BATCH * 128
+    per_group = 128 // BATCH
+
+    def copies(step, slot):
+        for b in range(BATCH):
+            block = info[1 + step * BATCH + b]
+            yield pltpu.make_async_copy(
+                emb.at[:, pl.ds(pl.multiple_of(block * 128, 128), 128)],
+                buf.at[slot, :, pl.ds(b * 128, 128)],
+                sems.at[slot, b],
+            )
+
+    acc[...] = jnp.zeros_like(acc)
+
+    @pl.when(rounds > 0)
+    def _():
+        for copy in copies(0, 0):
+            copy.start()
+
+    def body(step, carry):
+        slot = lax.rem(step, 2)
+        group = step // per_group
+        within = step - group * per_group
+
+        @pl.when(step + 1 < rounds)
+        def _():
+            for copy in copies(step + 1, 1 - slot):
+                copy.start()
+
+        for copy in copies(step, slot):
+            copy.wait()
+        lane = lanes[pl.ds(group, 1), :]
+        at = lax.broadcasted_iota(jnp.int32, lane.shape, 1) - within * BATCH
+        rel = jnp.where((lane >= 0) & (at >= 0) & (at < BATCH), at * 128 + lane, -1)
+        hot = lax.broadcasted_iota(jnp.int32, (width, 128), 0) == rel
+        got = jnp.dot(buf[slot], hot.astype(jnp.bfloat16), preferred_element_type=jnp.float32)
+
+        @pl.when(within == 0)
+        def _():
+            held[...] = got
+
+        @pl.when(within > 0)
+        def _():
+            held[...] += got
+
+        @pl.when((within == per_group - 1) | (step == rounds - 1))
+        def _():
+            name = listed[pl.ds(pl.multiple_of(group * 128, 128), 128), :]
+            spread = (name == ids[...]).astype(jnp.bfloat16)
+            acc[...] += jnp.dot(
+                held[...].astype(jnp.bfloat16), spread, preferred_element_type=jnp.float32
+            )
+
+        return carry
+
+    lax.fori_loop(0, rounds, body, 0)
+    out[...] = acc[...].astype(jnp.bfloat16)
+
+
+def pick_rows(emb_t, flat_ids, vocab_start):
+    width, vocab = emb_t.shape
+    rows = flat_ids.shape[0]
+    ids = flat_ids - vocab_start
+    ids = jnp.where((ids >= 0) & (ids < vocab), ids, -2)
+    number = jnp.arange(rows, dtype=jnp.int32)
+    same = (ids[:, None] == ids[None, :]) & (number[:, None] < number[None, :])
+    first = (ids >= 0) & ~jnp.any(same, axis=0)
+    rank = jnp.sum(
+        jnp.where((number[:, None] < number[None, :]) & first[:, None], 1, 0), axis=0
+    )
+    listed = jnp.max(
+        jnp.where(first[None, :] & (rank[None, :] == number[:, None]), ids[None, :], -1),
+        axis=1,
+    )
+    count = jnp.sum(first.astype(jnp.int32))
+    info = jnp.concatenate(
+        [count[None], jnp.maximum(listed, 0) >> 7, jnp.zeros((BATCH,), jnp.int32)]
+    )
+    lanes = jnp.where(listed >= 0, listed & 127, -1).reshape(rows // 128, 128)
+    return pl.pallas_call(
+        pick_kernel,
+        out_shape=jax.ShapeDtypeStruct((width, rows), jnp.bfloat16),
+        in_specs=[SMEM, ANY, VMEM, VMEM, VMEM],
+        out_specs=VMEM,
+        scratch_shapes=[
+            pltpu.VMEM((2, width, BATCH * 128), jnp.bfloat16),
+            pltpu.VMEM((width, 128), jnp.float32),
+            pltpu.VMEM((width, rows), jnp.float32),
+            pltpu.SemaphoreType.DMA((2, BATCH)),
+        ],
+        name="pick_rows",
+    )(info, emb_t, lanes, listed[:, None], ids[None, :])
+
+
+def padded(width):
+    return -(-width // 128) * 128
+
+
+def norm_kernel(pos, gain, x, out):
+    n, width, rows = x.shape
+    pitch = padded(width)
+    step = 128
+    pieces = [(at, min(step, width - at)) for at in range(0, width, step)]
+
+    def squares(r, total):
+        for at, size in pieces:
+            block = x[r, at : at + size, :].astype(jnp.float32)
+            total = total + jnp.sum((block * block).reshape(size // 8, 8, rows), axis=0)
+        return total
+
+    total = lax.fori_loop(0, n, squares, jnp.zeros((8, rows), jnp.float32))
+    mean_sq = jnp.sum(total, axis=0, keepdims=True) / (n * width)
+    scale = lax.rsqrt(mean_sq + eps_norm)
+    for r in range(n):
+        for at, size in pieces:
+            block = x[r, at : at + size, :].astype(jnp.float32) * scale
+            block = block.T * gain[r : r + 1, at : at + size]
+            out[:, r * pitch + at : r * pitch + at + size] = block.astype(jnp.bfloat16)
+
+
+def norm_rows(pos, gain, x):
+    n, width, rows = x.shape
+    return pl.pallas_call(
+        norm_kernel,
+        out_shape=jax.ShapeDtypeStruct((rows, n * padded(width)), jnp.bfloat16),
+        in_specs=[SMEM, VMEM, VMEM],
+        out_specs=VMEM,
+        name="norm_rows",
+    )(pos, gain, x)
+
+
+def piece_copies(grp, pieces, store, sems):
+    own, core, near, far = pieces
+    rows = own.shape[0]
+    part = rows // len(near)
+    groups = [
+        [pltpu.make_async_copy(own, store.at[0], sems.at[0])],
+        [pltpu.make_async_copy(core, store.at[1], sems.at[1])],
+    ]
+    at = 2
+    for r, blocks in ((2, near), (3, far)):
+        group = []
+        for i, block in enumerate(blocks):
+            half = grp if i % 2 == 0 else 1 - grp
+            start = pl.multiple_of(half * (rows // 2) + (i // 2) * part, 16)
+            group.append(
+                pltpu.make_async_copy(block, store.at[r, pl.ds(start, part), :], sems.at[at])
+            )
+            at += 1
+        groups.append(group)
+    return groups
+
+
+def proj_kernel(normed_cols, count, parts, pos, gain, cosine, sine, *refs):
+    sources, refs = refs[:count], refs[count:]
+    near, far = refs[2 : 2 + parts], refs[2 + parts : 2 + 2 * parts]
+    out, x, store, total, x_sems, w_sems = refs[2 + 2 * parts :]
+    groups = piece_copies(pos[2], (refs[0], refs[1], near, far), store, w_sems)
+    width, pitch = store.shape[1], x.shape[2]
+    loads = []
+    for r in range(4):
+        at = 0
+        slot = pl.multiple_of(lax.bitwise_xor(pos[0], r) * pitch, 128)
+        for i, source in enumerate(sources):
+            rows = source.shape[0]
+            loads.append(
+                pltpu.make_async_copy(
+                    source.at[:, pl.ds(slot, pitch)], x.at[r, pl.ds(at, rows), :], x_sems.at[r, i]
+                )
+            )
+            loads[-1].start()
+            at += rows
+        for copy in groups[r]:
+            copy.start()
+    head = gain.shape[1]
+    for r in range(4):
+        for copy in loads[r * count : (r + 1) * count] + groups[r]:
+            copy.wait()
+        part = jnp.dot(x[r, :, :width], store[r], preferred_element_type=jnp.float32)
+        if r == 0:
+            total[...] = part
+        else:
+            total[...] += part
+    for start in range(0, out.shape[1], head):
+        value = total[:, start : start + head]
+        if start < normed_cols:
+            mean_sq = jnp.mean(value * value, axis=-1, keepdims=True)
+            value = value * lax.rsqrt(mean_sq + eps_norm) * gain[...]
+            turned = pltpu.roll(value, head // 2, 1)
+            value = value * cosine[...] + turned * sine[...]
+        out[:, start : start + head] = value.astype(jnp.bfloat16)
+
+
+def project(normed_cols, pos, sources, gain, cosine, sine, pieces):
+    own, core, near, far = pieces
+    width, columns = own.shape
+    rows = sum(source.shape[0] for source in sources)
+    return pl.pallas_call(
+        functools.partial(proj_kernel, normed_cols, len(sources), len(near)),
+        out_shape=jax.ShapeDtypeStruct((rows, columns), jnp.bfloat16),
+        in_specs=[SMEM] + [VMEM] * 3 + [ANY] * (len(sources) + 2 + 2 * len(near)),
+        out_specs=VMEM,
+        scratch_shapes=[
+            pltpu.VMEM((4, rows, padded(width)), jnp.bfloat16),
+            pltpu.VMEM((4, width, columns), jnp.bfloat16),
+            pltpu.VMEM((rows, columns), jnp.float32),
+            pltpu.SemaphoreType.DMA((4, len(sources))),
+            pltpu.SemaphoreType.DMA((2 + 2 * len(near),)),
+        ],
+        name="project",
+    )(pos, gain[None, :], cosine, sine, *sources, own, core, *near, *far)
+
+
+def softmax_mix(scores, scale, values):
+    top = jnp.max(scores, axis=-1, keepdims=True)
+    weights = jnp.exp((scores - top) * scale)
+    total = jnp.sum(weights, axis=-1, keepdims=True)
+    weights = (weights / total).astype(jnp.bfloat16)
+    return jnp.dot(weights, values, preferred_element_type=jnp.float32)
+
+
+def stacked(source, head):
+    count = source.shape[1] // head
+    return jnp.concatenate([source[:, g * head : (g + 1) * head] for g in range(count)], axis=0)
+
+
+def unstack(mixed, out, head):
+    rows = out.shape[1]
+    for g in range(out.shape[2] // head):
+        out[0, :, g * head : (g + 1) * head] = mixed[g * rows : (g + 1) * rows].astype(
+            jnp.bfloat16
+        )
+
+
+CONTRACT = (((1,), (1,)), ((), ()))
+
+
+def prompt_kernel(pos, q, k0, k2, v0, v2, out):
+    own_index = pos[0]
+    block = lax.bitwise_xor(own_index, pl.program_id(1))
+    tokens, head = q.shape[0], k0.shape[1]
+    keys = [k0[:tokens], k0[tokens:], k2[:tokens], k2[tokens:]]
+    q_own = stacked(q, head)
+    rows = q_own.shape[0]
+    q_at = lax.rem(lax.broadcasted_iota(jnp.int32, (rows, tokens), 0), tokens)
+    ahead = q_at - lax.broadcasted_iota(jnp.int32, (rows, tokens), 1)
+    blocks = []
+    for r in range(4):
+        gap = ahead + (block - lax.bitwise_xor(own_index, r)) * tokens
+        score = lax.dot_general(q_own, keys[r], CONTRACT, preferred_element_type=jnp.float32)
+        blocks.append(jnp.where((gap >= 0) & (gap < WINDOW), score, -1e30))
+    values = jnp.concatenate([v0[...], v2[...]], axis=0)
+    scale = query_scalar ** (-0.5)
+    unstack(softmax_mix(jnp.concatenate(blocks, axis=1), scale, values), out, head)
+
+
+def cont_kernel(cont_len, tokens, pos, q, k0, k2, v0, v2, ck, cv, out):
+    own_index = pos[0]
+    conts, head = q.shape[0], k0.shape[1]
+    keys = [k0[:tokens], k0[tokens:], k2[:tokens], k2[tokens:]]
+    q_cont = stacked(q, head)
+    rows = q_cont.shape[0]
+    q_row = lax.rem(lax.broadcasted_iota(jnp.int32, (rows, tokens), 0), conts)
+    late = lax.broadcasted_iota(jnp.int32, (rows, tokens), 1) - lax.rem(q_row, cont_len)
+    blocks = []
+    for r in range(4):
+        base = lax.bitwise_xor(own_index, r) * tokens - (4 * tokens - WINDOW)
+        score = lax.dot_general(q_cont, keys[r], CONTRACT, preferred_element_type=jnp.float32)
+        blocks.append(jnp.where(late + base > 0, score, -1e30))
+    q_row = lax.rem(lax.broadcasted_iota(jnp.int32, (rows, conts), 0), conts)
+    k_row = lax.broadcasted_iota(jnp.int32, (rows, conts), 1)
+    same = (q_row // cont_len) == (k_row // cont_len)
+    score = lax.dot_general(q_cont, ck[...], CONTRACT, preferred_element_type=jnp.float32)
+    blocks.append(jnp.where(same & (k_row <= q_row), score, -1e30))
+    values = jnp.concatenate([v0[...], v2[...], cv[...]], axis=0)
+    scale = query_scalar ** (-0.5)
+    unstack(softmax_mix(jnp.concatenate(blocks, axis=1), scale, values), out, head)
+
+
+def attend_rows(kernel, head, pos, queries, here_kv, there_kv, cont_kv):
+    rows, q_cols = queries.shape[0] // 2, queries.shape[1]
+    span = here_kv.shape[0]
+    kv_heads = here_kv.shape[1] // (2 * head)
+    wide = q_cols // kv_heads
+
+    def column(shift):
+        return pl.BlockSpec((span, head), lambda h, b, pos: (0, h + shift))
+
+    def cont_column(shift):
+        return pl.BlockSpec((rows, head), lambda h, b, pos: (b, h + shift))
+
+    specs = [pl.BlockSpec((rows, wide), lambda h, b, pos: (b, h))]
+    specs += [column(0), column(0), column(kv_heads), column(kv_heads)]
+    operands = [queries, here_kv, there_kv, here_kv, there_kv]
+    if cont_kv is not None:
+        specs += [cont_column(0), cont_column(kv_heads)]
+        operands += [cont_kv, cont_kv]
+    return pl.pallas_call(
+        kernel,
+        out_shape=jax.ShapeDtypeStruct((2, rows, q_cols), jnp.bfloat16),
+        grid_spec=pltpu.PrefetchScalarGridSpec(
+            num_scalar_prefetch=1,
+            grid=(kv_heads, 2),
+            in_specs=specs,
+            out_specs=pl.BlockSpec((1, rows, wide), lambda h, b, pos: (b, 0, h)),
+        ),
+        name="attend_rows",
+    )(pos, *operands)
+
+
+def out_kernel(parts, pos, mine, theirs, *refs):
+    seq_index, grp = pos[0], pos[2]
+    core = lax.bitwise_and(seq_index, 1)
+    near, far = refs[2 : 2 + parts], refs[2 + parts : 2 + 2 * parts]
+    out, mixed, turned, store, m_sems, sems = refs[2 + 2 * parts :]
+    groups = piece_copies(grp, (refs[0], refs[1], near, far), store, sems)
+    half = mine.shape[1]
+    loads = []
+    for i, (source, side) in enumerate(((mine, core), (theirs, 1 - core))):
+        columns = pl.ds(pl.multiple_of(side * half, 128), half)
+        loads.append(pltpu.make_async_copy(source, mixed.at[:, columns], m_sems.at[i]))
+        loads[i].start()
+    for group in groups:
+        for copy in group:
+            copy.start()
+    for copy in loads:
+        copy.wait()
+    turned[...] = mixed[...].T
+    for r in range(4):
+        for copy in groups[r]:
+            copy.wait()
+        slot = lax.bitwise_xor(seq_index, r)
+        size = store.shape[1] // 4
+        for at in range(0, store.shape[1], size):
+            out[slot, at : at + size] = jnp.dot(
+                store[r, at : at + size], turned[...], preferred_element_type=jnp.float32
+            ).astype(jnp.bfloat16)
+
+
+def project_out(pos, mine, theirs, pieces):
+    own, core, near, far = pieces
+    width, size = own.shape
+    rows = mine.shape[0]
+    return pl.pallas_call(
+        functools.partial(out_kernel, len(near)),
+        out_shape=jax.ShapeDtypeStruct((4, width, rows), jnp.bfloat16),
+        in_specs=[SMEM] + [ANY] * (4 + 2 * len(near)),
+        out_specs=VMEM,
+        scratch_shapes=[
+            pltpu.VMEM((rows, size), jnp.bfloat16),
+            pltpu.VMEM((size, rows), jnp.bfloat16),
+            pltpu.VMEM((4, width, size), jnp.bfloat16),
+            pltpu.SemaphoreType.DMA((2,)),
+            pltpu.SemaphoreType.DMA((2 + 2 * len(near),)),
+        ],
+        name="project_out",
+    )(pos, mine, theirs, own, core, *near, *far)
+
+
+def line_scatter(parts, axis):
+    count = lax.axis_size(axis)
+    index = lax.axis_index(axis)
+
+    def block(at):
+        return lax.dynamic_index_in_dim(parts, jnp.clip(at, 0, count - 1), 0, False)
+
+    a = b = None
+    for step in range(1, count):
+        far = count - step
+        send_a, send_b = block(index + far), block(index - far)
+        if a is not None:
+            send_a = (send_a.astype(jnp.float32) + a.astype(jnp.float32)).astype(jnp.bfloat16)
+            send_b = (send_b.astype(jnp.float32) + b.astype(jnp.float32)).astype(jnp.bfloat16)
+        a = lax.ppermute(send_a, axis, [(i, i + 1) for i in range(step)])
+        b = lax.ppermute(send_b, axis, [(count - 1 - i, count - 2 - i) for i in range(step)])
+    return (
+        block(index).astype(jnp.float32) + a.astype(jnp.float32) + b.astype(jnp.float32)
+    )
+
+
+def total_over(value, axis):
+    count = lax.axis_size(axis)
+    total = value
+    for by in range(1, count):
+        pairs = [(i, (i + by) % count) for i in range(count)]
+        total = total + lax.ppermute(value, axis, pairs)
+    return total
+
+
+def swap(by):
+    return [(i, i ^ by) for i in range(lax.axis_size("seq"))]
+
+
+ACROSS = [(0, 1), (1, 0)]
+
+
+def half_pieces(mine, other):
+    half = mine.shape[0] // 2
+    start = lax.axis_index("grp") * half
+    near = lax.ppermute(lax.dynamic_slice_in_dim(mine, start, half), "seq", swap(2))
+    far = lax.ppermute(lax.dynamic_slice_in_dim(other, start, half), "seq", swap(3))
+    core = lax.ppermute(other, "seq", swap(1))
+    near_x = lax.ppermute(near, "grp", ACROSS)
+    far_x = lax.ppermute(far, "grp", ACROSS)
+    return mine, core, [near, near_x], [far, far_x]
+
+
+def full_pieces(weight, chunks):
+    half = weight.shape[0] // 2
+    part = half // chunks
+    near, far = [], []
+    core = lax.ppermute(weight, "seq", swap(1))
+    for i in range(chunks):
+        start = lax.axis_index("grp") * half + i * part
+        mine = lax.dynamic_slice_in_dim(weight, start, part)
+        got = lax.ppermute(mine, "seq", swap(2))
+        more = lax.ppermute(got, "grp", ACROSS)
+        near += [got, more]
+        far += [lax.ppermute(got, "seq", swap(1)), lax.ppermute(more, "seq", swap(1))]
+    return weight, core, near, far
+
+
+def on_device(*args):
+    return paired_device(*args)
+
+
+def paired_device(
+    prompt, cont_ids, embed, pre_gain, w_query, w_keyval, q_gain, k_gain, w_out, post_gain
+):
+    tok_rows, local_cols = prompt.shape
+    n_seq = lax.axis_size("seq")
+    n_tp = lax.axis_size("tp")
+    seq_index = lax.axis_index("seq")
+    tp_index = lax.axis_index("tp")
+    core_index = seq_index & 1
+    full_width = local_cols * n_tp
+    cont_count, cont_len = cont_ids.shape
+    own_conts = cont_count // n_seq
+    cont_rows = own_conts * cont_len
+    head_dim = q_gain.shape[0]
+    pos = jnp.stack([seq_index, tp_index, lax.axis_index("grp")]).astype(jnp.int32)
+
+    prompt_t = prompt.T
+    prompt_x = lax.all_gather(prompt_t, "tp", axis=0)
+
+    def half_of(weight, side):
+        size = weight.shape[-1] // 2
+        part = lax.dynamic_slice_in_dim(weight, side * size, size, weight.ndim - 1)
+        return part.reshape(part.shape[0], -1)
+
+    kv_pieces = half_pieces(half_of(w_keyval, core_index), half_of(w_keyval, 1 - core_index))
+    q_pieces = half_pieces(half_of(w_query, core_index), half_of(w_query, 1 - core_index))
+    out_pieces = full_pieces(w_out.T, 2)
+
+    ids = cont_ids.reshape(n_seq, cont_rows)
+    held = []
+    for parts in ((1, 3), (0, 2)):
+        wanted = [lax.dynamic_index_in_dim(ids, seq_index ^ r, 0, False) for r in parts]
+        start = seq_index * embed.shape[0]
+        held.append(pick_rows(embed.T, jnp.concatenate(wanted), start))
+    give, keep = held
+    keep = keep + lax.ppermute(give, "seq", swap(1))
+    mine = keep[:, :cont_rows] + lax.ppermute(keep[:, cont_rows:], "seq", swap(2))
+    cont_t = (mine.astype(jnp.float32) * math.sqrt(full_width)).astype(jnp.bfloat16)
+    cont_x = lax.all_gather(cont_t, "tp", axis=0)
+
+    def turns(positions):
+        lane = jnp.arange(head_dim, dtype=jnp.int32)
+        half = head_dim // 2
+        freqs = rope_base ** (-((lane % half).astype(jnp.float32) * 2.0) / head_dim)
+        angles = positions.astype(jnp.float32)[:, None] * freqs[None, :]
+        return jnp.cos(angles), jnp.sin(angles) * jnp.where(lane < half, -1.0, 1.0)
+
+    row = jnp.arange(2 * tok_rows, dtype=jnp.int32)
+    block = jnp.where(row < tok_rows, seq_index, seq_index ^ 1)
+    prompt_turns = turns(block * tok_rows + row % tok_rows)
+    spot = jnp.arange(2 * cont_rows, dtype=jnp.int32) % cont_len
+    cont_turns = turns(n_seq * tok_rows + spot)
+
+    gain = pre_gain.reshape(n_tp, local_cols)
+    kv_cols = w_keyval.shape[2] // 2
+    q_cols = w_query.shape[1] // 2
+
+    def rows_of(x):
+        normed = norm_rows(pos, gain, x)
+        return [normed, lax.ppermute(normed, "seq", swap(1))]
+
+    def shares(mixed):
+        return mixed[0], lax.ppermute(mixed[1], "seq", swap(1))
+
+    rows_p = rows_of(prompt_x)
+    here_kv = project(kv_cols, pos, rows_p, k_gain, *prompt_turns, kv_pieces)
+    there_kv = lax.ppermute(here_kv, "seq", swap(2))
+    queries_p = project(q_cols, pos, rows_p, q_gain, *prompt_turns, q_pieces)
+    mixed_p = attend_rows(prompt_kernel, head_dim, pos, queries_p, here_kv, there_kv, None)
+    pair_p = shares(mixed_p)
+    rows_c = rows_of(cont_x)
+    cont_kv = project(kv_cols, pos, rows_c, k_gain, *cont_turns, kv_pieces)
+    queries_c = project(q_cols, pos, rows_c, q_gain, *cont_turns, q_pieces)
+    kernel = functools.partial(cont_kernel, cont_len, tok_rows)
+    mixed_c = attend_rows(kernel, head_dim, pos, queries_c, here_kv, there_kv, cont_kv)
+    pair_c = shares(mixed_c)
+    part_p = project_out(pos, *pair_p, out_pieces)
+    part_c = project_out(pos, *pair_c, out_pieces)
+    gain_part = lax.dynamic_slice_in_dim(post_gain, tp_index * local_cols, local_cols)[:, None]
+
+    attn_p = lax.psum_scatter(part_p, "tp", scatter_dimension=0).astype(jnp.float32)
+    attn_c = line_scatter(part_c, "tp")
+    row_sq = jnp.concatenate(
+        [jnp.sum(attn * attn, axis=0, keepdims=True) for attn in (attn_p, attn_c)], axis=1
+    )
+    factor = lax.rsqrt(total_over(row_sq, "tp") / full_width + eps_norm)
+
+    def finish(attn, factor, rows_t):
+        return (rows_t.astype(jnp.float32) + attn * factor * gain_part).astype(jnp.bfloat16)
+
+    prompt_out = finish(attn_p, factor[:, :tok_rows], prompt_t).T
+    cont_out = finish(attn_c, factor[:, tok_rows:], cont_t).T
+    return (prompt_out, cont_out.reshape(own_conts, cont_len, local_cols))
+
+
 def solution(mesh):
+    shape = mesh.shape
+    paired = shape["grp"] == 2 and shape["seq"] == 4 and shape["tp"] == 4
     return jax.shard_map(
-        on_device,
+        on_device if paired else plain_device,
         mesh=mesh,
         in_specs=(
             P(("grp", "seq"), "tp"),

time: 662 us -> 362 us (0.55)
  waiting for transfers between devices: 364 us -> 156 us
  local copies, waits for them, and re-layouts: 144 us -> 28.5 us
  Pallas kernels: 0 us -> 100 us
  matrix products: 53.3 us -> 0 us
  blocking collectives: 11 us -> 0 us
  other arithmetic: 24.2 us -> 17.4 us
    all_gather x4 -> x2, waiting for transfers between devices: 228 us -> 23 us  [the longest x1 23 us: paired_device(): prompt_x = lax.all_gather(prompt_t, 'tp', axis=0)]
    ppermute x4 -> x35, waiting for transfers between devices: 5.22 us -> 133 us  [the longest x2 26.8 us: full_pieces(): more = lax.ppermute(got, 'grp', ACROSS)]
    unnamed x45 -> x34, local copies, waits for them, and re-layouts: 113 us -> 5.12 us
    pallas_call x0 -> x12, Pallas kernels: none -> 100 us  [the longest x4 28.8 us: project(): pl.pallas_call(functools.partial(proj_kernel, normed_cols, len(sources),...]
    reduce_scatter x1, waiting for transfers between devices: 75 us -> 0.01 us  [paired_device(): lax.psum_scatter(part_p, 'tp', scatter_dimension=0).astype(jnp.float32)]
    dot_general x5 -> x0, matrix products: 42.5 us -> none  [the longest x1 11.5 us: on_device(): jnp.dot(mixed, lax.all_gather(w_out, 'seq', axis=1, tiled=True), preferre...]
    unnamed x8 -> x3, waiting for transfers between devices: 30.9 us -> 0.71 us
    psum x1 -> x0, waiting for transfers between devices: 24.6 us -> none  [from_root(): return lax.psum(jnp.where(mine, value, jnp.zeros_like(value)), axis)]
  transfers between devices with their start and end apart: 11 -> 38, of which waited for: 10 -> 17; matrix products, arithmetic and copies ran while one was open for 11% -> 10% of each run, Pallas kernels for 0% -> 28%
where the time goes in v1:
time: 362 us; the launch traced here: 361 us
  waiting for transfers between devices  156 us (43%)
  Pallas kernels  100 us (28%)
  starting transfers between devices  44.3 us (12%)
  local copies, waits for them, and re-layouts  28.5 us (8%)
  other arithmetic  17.4 us (5%)
  between operations  14.2 us (4%)
    pallas_call x4, Pallas kernels, project(): pl.pallas_call(functools.partial(proj_kernel, normed_cols, len(sources),...  28.8 us
    ppermute x2, waiting for transfers between devices, full_pieces(): more = lax.ppermute(got, 'grp', ACROSS)  26.8 us
    pallas_call x2, Pallas kernels, pick_rows(): pl.pallas_call(pick_kernel, out_shape=jax.ShapeDtypeStruct((width, rows),...  25.6 us
    ppermute x3, waiting for transfers between devices, line_scatter(): a = lax.ppermute(send_a, axis, [(i, i + 1) for i in range(step)])  24.5 us
    all_gather x1, waiting for transfers between devices, paired_device(): prompt_x = lax.all_gather(prompt_t, 'tp', axis=0)  23 us
    pallas_call x2, Pallas kernels, project_out(): pl.pallas_call(functools.partial(out_kernel, len(near)), out_shape=jax.Sh...  19.8 us
    pallas_call x2, Pallas kernels, attend_rows(): pl.pallas_call(kernel, out_shape=jax.ShapeDtypeStruct((2, rows, q_cols),...  17.1 us
    ppermute x2, waiting for transfers between devices, half_pieces(): near_x = lax.ppermute(near, 'grp', ACROSS)  15.3 us
  transfers between devices with their start and end apart: 38, of which 17 were waited for; matrix products, arithmetic and copies ran while one was open for 10% of the time, Pallas kernels for 28%

profile of v1, /device:TPU:0, one launch (start us, length us, event | category | flops | bytes accessed | tf_op | source)
XLA Modules:
  0.0 361.0 jit_solution(17930558337374111348)
XLA Ops:
  13.3 1.8 pad_add_fusion
  15.1 12.2 %pick_rows.3 = bf16[1344,256]{1,0:T(8,128)(2,1)} custom-call(s32[265]{0:T(512)} %get-tuple-element.36.info, bf16[1344,32768]{1,0:T(8,128)(2,1)} %bitcast.18.emb, s32[2,128]{1,0:T(2,128)} %get-tuple-element.32.lanes, s32[256,1]{1,0:T(8,128)} %copy.17.listed, s32[1,256]{1,0:T(1,128)} %and_select_fusion.ids), custom_call_target="tpu_custom_call" | custom-call | tf_op jit(solution)/shard_map/pick_rows/pallas_call | solution.py:273
  27.3 2.4 collective-permute-start.22
  29.7 3.6 constant_dynamic-slice_fusion.6
  33.6 1.0 constant_dynamic-slice_fusion.5
  34.6 6.8 %collective-permute-start.7 = (bf16[672,512]{1,0:T(8,128)(2,1)}, bf16[672,512]{1,0:T(8,128)(2,1)S(1)}, u32[]{:S(2)}, u32[]{:S(2)}) collective-permute-start(bf16[672,512]{1,0:T(8,128)(2,1)} %constant_dynamic-slice_fusion.5), channel_id=1, source_target_pairs={{0,8},{4,12},{8,0},{12,4},{1,9},{5,13},{9,1},{13,5},{2,10},{6,14},... | collective-permute-start | bytes 2064392 | tf_op jit(solution)/shard_map/ppermute | solution.py:593
  41.5 1.4 copy.20
  42.9 2.0 constant_dynamic-slice_fusion.4
  46.2 23.0 %all-gather.5.cloned.1.call-done = bf16[5376,256]{1,0:T(8,128)(2,1)} async-done(((bf16[1344,256]{1,0:T(8,128)(2,1)}), bf16[5376,256]{1,0:T(8,128)(2,1)}) %all-gather.5.cloned.1.call-update) | async-done | bytes 2752528 | tf_op jit(solution)/shard_map/all_gather | solution.py:637
  69.2 5.1 %norm_rows.2.refs_0_ = bf16[256,5632]{1,0:T(8,128)(2,1)} custom-call(s32[3]{0:T(128)} %pad_add_fusion.2.pos, f32[4,1344]{1,0:T(4,128)} %reshape.287.gain, bf16[4,1344,256]{2,1,0:T(8,128)(2,1)} %bitcast.81), custom_call_target="tpu_custom_call" | custom-call | tf_op jit(solution)/shard_map/norm_rows/pallas_call | solution.py:316
  74.3 3.4 fusion.35
  77.7 1.5 collective-permute-start.2
  79.2 0.9 dynamic-slice_bitcast_fusion
  80.9 1.5 collective-permute-start.14
  82.9 13.4 %collective-permute-done.2.refs_4_ = bf16[672,512]{1,0:T(8,128)(2,1)} collective-permute-done((bf16[672,512]{1,0:T(8,128)(2,1)}, bf16[672,512]{1,0:T(8,128)(2,1)}, u32[]{:S(2)}, u32[]{:S(2)}) %collective-permute-start.2) | collective-permute-done | bytes 688160 | tf_op jit(solution)/shard_map/ppermute | solution.py:593
  96.3 13.8 %collective-permute-done.4.refs_6_ = bf16[672,512]{1,0:T(8,128)(2,1)} collective-permute-done((bf16[672,512]{1,0:T(8,128)(2,1)S(1)}, bf16[672,512]{1,0:T(8,128)(2,1)}, u32[]{:S(2)}, u32[]{:S(2)}) %collective-permute-start.4) | collective-permute-done | bytes 688160 | tf_op jit(solution)/shard_map/ppermute | solution.py:594
  110.1 1.5 collective-permute-start.8
  111.6 14.2 %collective-permute-done.14.refs_2_ = bf16[336,1024]{1,0:T(8,128)(2,1)} collective-permute-done((bf16[336,1024]{1,0:T(8,128)(2,1)S(1)}, bf16[336,1024]{1,0:T(8,128)(2,1)}, u32[]{:S(2)}, u32[]{:S(2)}) %collective-permute-start.14) | collective-permute-done | bytes 688160 | tf_op jit(solution)/shard_map/ppermute | solution.py:609
  125.8 1.5 collective-permute-start.10
  128.7 13.4 %pick_rows.2 = bf16[1344,256]{1,0:T(8,128)(2,1)} custom-call(s32[265]{0:T(512)} %get-tuple-element.37.info, bf16[1344,32768]{1,0:T(8,128)(2,1)} %bitcast.18.emb, s32[2,128]{1,0:T(2,128)} %get-tuple-element.34.lanes, s32[256,1]{1,0:T(8,128)} %copy.16.listed, s32[1,256]{1,0:T(1,128)} %and_select_fusion.1.ids), custom_call_target="tpu_custom_call" | custom-call | tf_op jit(solution)/shard_map/pick_rows/pallas_call | solution.py:273
  142.1 1.6 add.200
  143.8 1.7 collective-permute-start.23
  145.5 7.2 %collective-permute-done.23 = bf16[1344,128]{1,0:T(8,128)(2,1)S(1)} collective-permute-done((bf16[1344,128]{1,0:T(8,128)(2,1)S(1)}, bf16[1344,128]{1,0:T(8,128)(2,1)S(1)}, u32[]{:S(2)}, u32[]{:S(2)}) %collective-permute-start.23) | collective-permute-done | bytes 344096 | tf_op jit(solution)/shard_map/ppermute | solution.py:656
  152.7 2.0 constant_dynamic-slice_fusion.8
  155.9 0.8 multiply_convert_fusion
  157.0 1.4 collective-permute-start.5
  158.4 15.3 %collective-permute-done.3.refs_5_ = bf16[672,512]{1,0:T(8,128)(2,1)S(1)} collective-permute-done((bf16[672,512]{1,0:T(8,128)(2,1)}, bf16[672,512]{1,0:T(8,128)(2,1)S(1)}, u32[]{:S(2)}, u32[]{:S(2)}) %collective-permute-start.3) | collective-permute-done | bytes 688160 | tf_op jit(solution)/shard_map/ppermute | solution.py:596
  174.4 1.3 collective-permute-start.17
  175.8 1.8 fusion.11
  177.6 8.1 %project.5.k0.v0 = bf16[512,512]{1,0:T(8,128)(2,1)} custom-call(s32[3]{0:T(128)} %pad_add_fusion.2.pos, f32[1,128]{1,0:T(1,128)} %bitcast.96, f32[512,128]{1,0:T(8,128)} %get-tuple-element.25.cosine, f32[512,128]{1,0:T(8,128)} %get-tuple-element.24.sine, bf16[256,5632]{1,0:T(8,128)(2,1)} %norm_rows.2.refs_0_, ...), custom_call_target="tpu_custom_call" | custom-call | tf_op jit(solution)/shard_map/project/pallas_call | solution.py:391
  185.7 2.9 collective-permute-done.5.refs_7_
  188.6 1.7 collective-permute-start.11
  190.3 13.0 %collective-permute-done.15.refs_3_ = bf16[336,1024]{1,0:T(8,128)(2,1)} collective-permute-done((bf16[336,1024]{1,0:T(8,128)(2,1)}, bf16[336,1024]{1,0:T(8,128)(2,1)}, u32[]{:S(2)}, u32[]{:S(2)}) %collective-permute-start.15) | collective-permute-done | bytes 688160 | tf_op jit(solution)/shard_map/ppermute | solution.py:610
  203.3 13.8 %collective-permute-done.17.refs_5_ = bf16[336,1024]{1,0:T(8,128)(2,1)} collective-permute-done((bf16[336,1024]{1,0:T(8,128)(2,1)}, bf16[336,1024]{1,0:T(8,128)(2,1)}, u32[]{:S(2)}, u32[]{:S(2)}) %collective-permute-start.17) | collective-permute-done | bytes 688160 | tf_op jit(solution)/shard_map/ppermute | solution.py:610
  217.7 8.7 %project.4.q = bf16[512,512]{1,0:T(8,128)(2,1)} custom-call(s32[3]{0:T(128)} %pad_add_fusion.2.pos, f32[1,128]{1,0:T(1,128)} %bitcast.98, f32[512,128]{1,0:T(8,128)} %get-tuple-element.25.cosine, f32[512,128]{1,0:T(8,128)} %get-tuple-element.24.sine, bf16[256,5632]{1,0:T(8,128)(2,1)} %norm_rows.2.refs_0_, bf16[256,5632]{1,0:T(8,128)(2,1)} %collective-permute-done.refs_1_, ...), custom_call_target="tpu_custom_call" | custom-call | tf_op jit(solution)/shard_map/project/pallas_call | solution.py:391
  226.4 10.3 %attend_rows.2 = bf16[2,256,512]{2,1,0:T(8,128)(2,1)} custom-call(s32[3]{0:T(128)} %pad_add_fusion.2.pos, bf16[512,512]{1,0:T(8,128)(2,1)} %project.4.q, bf16[512,512]{1,0:T(8,128)(2,1)} %project.5.k0.v0, bf16[512,512]{1,0:T(8,128)(2,1)} %copy-done.3, bf16[512,512]{1,0:T(8,128)(2,1)} %project.5.k0.v0, bf16[512,512]{1,0:T(8,128)(2,1)} %copy-done.3), custom_call_target="tpu_custom_call" | custom-call | tf_op jit(solution)/shard_map/attend_rows/pallas_call | solution.py:491
  236.6 1.8 slice_bitcast_fusion
  238.6 1.3 collective-permute-done.12.theirs
  240.6 10.2 %project_out.2 = bf16[4,1344,256]{2,1,0:T(8,128)(2,1)} custom-call(s32[3]{0:T(128)} %pad_add_fusion.2.pos, bf16[256,512]{1,0:T(8,128)(2,1)} %get-tuple-element.21.mine, bf16[256,512]{1,0:T(8,128)(2,1)} %copy-done.13, bf16[1344,1024]{1,0:T(8,128)(2,1)} %bitcast.73, bf16[1344,1024]{1,0:T(8,128)(2,1)} %collective-permute-done.13.refs_1_, ...), custom_call_target="tpu_custom_call" | custom-call | tf_op jit(solution)/shard_map/project_out/pallas_call | solution.py:537
  250.9 3.8 %norm_rows.3.refs_0_ = bf16[128,5632]{1,0:T(8,128)(2,1)} custom-call(s32[3]{0:T(128)} %pad_add_fusion.2.pos, f32[4,1344]{1,0:T(4,128)} %reshape.287.gain, bf16[4,1344,128]{2,1,0:T(8,128)(2,1)} %bitcast.83), custom_call_target="tpu_custom_call" | custom-call | tf_op jit(solution)/shard_map/norm_rows/pallas_call | solution.py:316
  254.9 1.2 fusion.20
  256.2 2.0 collective-permute-done.24.refs_1_
  258.1 1.1 copy-done.5
  259.3 6.0 %project.7.ck.cv = bf16[256,512]{1,0:T(8,128)(2,1)} custom-call(s32[3]{0:T(128)} %pad_add_fusion.2.pos, f32[1,128]{1,0:T(1,128)} %bitcast.97, f32[256,128]{1,0:T(8,128)} %get-tuple-element.31.cosine, f32[256,128]{1,0:T(8,128)} %get-tuple-element.30.sine, bf16[128,5632]{1,0:T(8,128)(2,1)} %norm_rows.3.refs_0_, bf16[128,5632]{1,0:T(8,128)(2,1)} %copy-done.5, ...), custom_call_target="tpu_custom_call" | custom-call | tf_op jit(solution)/shard_map/project/pallas_call | solution.py:391
  265.3 6.1 %project.6.q = bf16[256,512]{1,0:T(8,128)(2,1)} custom-call(s32[3]{0:T(128)} %pad_add_fusion.2.pos, f32[1,128]{1,0:T(1,128)} %bitcast.99, f32[256,128]{1,0:T(8,128)} %get-tuple-element.31.cosine, f32[256,128]{1,0:T(8,128)} %get-tuple-element.30.sine, bf16[128,5632]{1,0:T(8,128)(2,1)} %norm_rows.3.refs_0_, bf16[128,5632]{1,0:T(8,128)(2,1)} %copy-done.5, ...), custom_call_target="tpu_custom_call" | custom-call | tf_op jit(solution)/shard_map/project/pallas_call | solution.py:391
  271.3 6.9 %attend_rows.3 = bf16[2,128,512]{2,1,0:T(8,128)(2,1)} custom-call(s32[3]{0:T(128)} %pad_add_fusion.2.pos, bf16[256,512]{1,0:T(8,128)(2,1)} %project.6.q, bf16[512,512]{1,0:T(8,128)(2,1)} %project.5.k0.v0, bf16[512,512]{1,0:T(8,128)(2,1)} %copy-done.3, bf16[512,512]{1,0:T(8,128)(2,1)} %project.5.k0.v0, bf16[512,512]{1,0:T(8,128)(2,1)} %copy-done.3, ...), custom_call_target="tpu_custom_call" | custom-call | tf_op jit(solution)/shard_map/attend_rows/pallas_call | solution.py:491
  278.2 1.6 slice_bitcast_fusion.2
  280.1 1.1 collective-permute-done.25.theirs
  281.9 9.6 %project_out.3 = bf16[4,1344,128]{2,1,0:T(8,128)(2,1)} custom-call(s32[3]{0:T(128)} %pad_add_fusion.2.pos, bf16[128,512]{1,0:T(8,128)(2,1)} %get-tuple-element.23.mine, bf16[128,512]{1,0:T(8,128)(2,1)} %copy-done.14, bf16[1344,1024]{1,0:T(8,128)(2,1)} %bitcast.74, bf16[1344,1024]{1,0:T(8,128)(2,1)} %collective-permute-done.13.refs_1_, ...), custom_call_target="tpu_custom_call" | custom-call | tf_op jit(solution)/shard_map/project_out/pallas_call | solution.py:537
  291.5 1.3 dynamic-slice_bitcast_fusion.3
  292.8 1.6 collective-permute-start.26
  295.0 12.0 %collective-permute-done.26 = bf16[1344,128]{1,0:T(8,128)(2,1)S(1)} collective-permute-done((bf16[1344,128]{1,0:T(8,128)(2,1)S(1)}, bf16[1344,128]{1,0:T(8,128)(2,1)S(1)}, u32[]{:S(2)}, u32[]{:S(2)}) %collective-permute-start.26) | collective-permute-done | bytes 344096 | tf_op jit(solution)/shard_map/ppermute | solution.py:567
  307.2 4.4 %collective-permute-start.27 = (bf16[1344,128]{1,0:T(8,128)(2,1)S(1)}, bf16[1344,128]{1,0:T(8,128)(2,1)S(1)}, u32[]{:S(2)}, u32[]{:S(2)}) collective-permute-start(bf16[1344,128]{1,0:T(8,128)(2,1)S(1)} %fusion.7), channel_id=1, source_target_pairs={{0,1},{1,2},{4,5},{5,6},{8,9},{9,10},{12,13},{13,14},{16,17},{17,1... | collective-permute-start | bytes 1032200 | tf_op jit(solution)/shard_map/ppermute | solution.py:567
  311.6 7.3 %collective-permute-done.27 = bf16[1344,128]{1,0:T(8,128)(2,1)S(1)} collective-permute-done((bf16[1344,128]{1,0:T(8,128)(2,1)S(1)}, bf16[1344,128]{1,0:T(8,128)(2,1)S(1)}, u32[]{:S(2)}, u32[]{:S(2)}) %collective-permute-start.27) | collective-permute-done | bytes 344096 | tf_op jit(solution)/shard_map/ppermute | solution.py:567
  319.8 5.1 %collective-permute-start.28 = (bf16[1344,128]{1,0:T(8,128)(2,1)S(1)}, bf16[1344,128]{1,0:T(8,128)(2,1)S(1)}, u32[]{:S(2)}, u32[]{:S(2)}) collective-permute-start(bf16[1344,128]{1,0:T(8,128)(2,1)S(1)} %get-tuple-element.16), channel_id=1, source_target_pairs={{0,1},{1,2},{2,3},{4,5},{5,6},{6,7},{8,9},{9,10},{10,11},{12,13},{... | collective-permute-start | bytes 1032200 | tf_op jit(solution)/shard_map/ppermute | solution.py:567
  325.1 1.3 collective-permute-start.31
  326.4 5.1 %collective-permute-done.28 = bf16[1344,128]{1,0:T(8,128)(2,1)S(1)} collective-permute-done((bf16[1344,128]{1,0:T(8,128)(2,1)S(1)}, bf16[1344,128]{1,0:T(8,128)(2,1)S(1)}, u32[]{:S(2)}, u32[]{:S(2)}) %collective-permute-start.28) | collective-permute-done | bytes 344096 | tf_op jit(solution)/shard_map/ppermute | solution.py:567
  331.5 9.5 %collective-permute-done.31 = bf16[1344,128]{1,0:T(8,128)(2,1)S(1)} collective-permute-done((bf16[1344,128]{1,0:T(8,128)(2,1)S(1)}, bf16[1344,128]{1,0:T(8,128)(2,1)S(1)}, u32[]{:S(2)}, u32[]{:S(2)}) %collective-permute-start.31) | collective-permute-done | bytes 344096 | tf_op jit(solution)/shard_map/ppermute | solution.py:568
  341.7 1.3 fusion
  343.0 1.8 collective-permute-start.32
  345.2 2.8 collective-permute-start.34
  349.4 2.0 fusion.10
  351.4 1.9 copy.18
  353.2 1.2 fusion.4
  (112 shorter events, 19.4 us)
Async XLA Ops:
  7.2 62.1 %all-gather.5.cloned.1.call-start = ((), (), s32[]{:S(2)}) async-start(), calls=%async_computation.2 | async-start | bytes 3440640 | tf_op jit(solution)/shard_map/all_gather | solution.py:637
  7.9 243.0 %all-gather.7.cloned.1.call-start = ((), (), s32[]{:S(2)}) async-start(), calls=%async_computation.3 | async-start | bytes 1720320 | tf_op jit(solution)/shard_map/all_gather | solution.py:658
  27.3 52.8 %collective-permute-start.22 = (bf16[1344,256]{1,0:T(8,128)(2,1)}, bf16[1344,256]{1,0:T(8,128)(2,1)}, u32[]{:S(2)}, u32[]{:S(2)}) collective-permute-start(bf16[1344,256]{1,0:T(8,128)(2,1)} %pick_rows.3), channel_id=1, source_target_pairs={{0,4},{4,0},{8,12},{12,8},{1,5},{5,1},{9,13},{13,9},{2,6},{6,2},{1... | collective-permute-start | bytes 2064392 | tf_op jit(solution)/shard_map/ppermute | solution.py:655
  33.6 9.2 %copy-start.1 = (bf16[168,8,2,256]{3,1,2,0:T(8,128)(2,1)}, bf16[168,8,2,256]{3,1,2,0:T(8,128)(2,1)S(1)}, u32[]{:S(2)}) copy-start(bf16[168,8,2,256]{3,1,2,0:T(8,128)(2,1)S(1)} %copy.19) | copy-start | bytes 4128772
  34.6 46.2 %collective-permute-start.7 = (bf16[672,512]{1,0:T(8,128)(2,1)}, bf16[672,512]{1,0:T(8,128)(2,1)S(1)}, u32[]{:S(2)}, u32[]{:S(2)}) collective-permute-start(bf16[672,512]{1,0:T(8,128)(2,1)} %constant_dynamic-slice_fusion.5), channel_id=1, source_target_pairs={{0,8},{4,12},{8,0},{12,4},{1,9},{5,13},{9,1},{13,5},{2,10},{6,14},... | collective-permute-start | bytes 2064392 | tf_op jit(solution)/shard_map/ppermute | solution.py:593
  42.9 2.1 copy-start.15
  44.9 37.5 %collective-permute-start.9 = (bf16[672,512]{1,0:T(8,128)(2,1)}, bf16[672,512]{1,0:T(8,128)(2,1)}, u32[]{:S(2)}, u32[]{:S(2)}) collective-permute-start(bf16[672,512]{1,0:T(8,128)(2,1)} %constant_dynamic-slice_fusion.4), channel_id=1, source_target_pairs={{0,12},{4,8},{8,4},{12,0},{1,13},{5,9},{9,5},{13,1},{2,14},{6,10},... | collective-permute-start | bytes 2064392 | tf_op jit(solution)/shard_map/ppermute | solution.py:594
  74.3 100.1 %collective-permute-start = (bf16[256,5632]{1,0:T(8,128)(2,1)}, bf16[256,5632]{1,0:T(8,128)(2,1)}, u32[]{:S(2)}, u32[]{:S(2)}) collective-permute-start(bf16[256,5632]{1,0:T(8,128)(2,1)} %norm_rows.2.refs_0_), channel_id=1, source_target_pairs={{0,4},{4,0},{8,12},{12,8},{1,5},{5,1},{9,13},{13,9},{2,6},{6,2},{1... | collective-permute-start | bytes 8650760 | tf_op jit(solution)/shard_map/ppermute | solution.py:679
  74.3 4.8 %copy-start = (bf16[1024,1344]{0,1:T(8,128)(2,1)S(1)}, bf16[1024,1344]{0,1:T(8,128)(2,1)}, u32[]{:S(2)}) copy-start(bf16[1024,1344]{0,1:T(8,128)(2,1)} %param.18) | copy-start | bytes 8257540
  77.7 18.6 %collective-permute-start.2 = (bf16[672,512]{1,0:T(8,128)(2,1)}, bf16[672,512]{1,0:T(8,128)(2,1)}, u32[]{:S(2)}, u32[]{:S(2)}) collective-permute-start(bf16[672,512]{1,0:T(8,128)(2,1)} %get-tuple-element.13), channel_id=1, source_target_pairs={{0,8},{4,12},{8,0},{12,4},{1,9},{5,13},{9,1},{13,5},{2,10},{6,14},... | collective-permute-start | bytes 2064392 | tf_op jit(solution)/shard_map/ppermute | solution.py:593
  79.2 1.3 copy-start.12
  80.5 29.6 %collective-permute-start.4 = (bf16[672,512]{1,0:T(8,128)(2,1)S(1)}, bf16[672,512]{1,0:T(8,128)(2,1)}, u32[]{:S(2)}, u32[]{:S(2)}) collective-permute-start(bf16[672,512]{1,0:T(8,128)(2,1)S(1)} %copy-done.12), channel_id=1, source_target_pairs={{0,12},{4,8},{8,4},{12,0},{1,13},{5,9},{9,5},{13,1},{2,14},{6,10},... | collective-permute-start | bytes 2064392 | tf_op jit(solution)/shard_map/ppermute | solution.py:594
  80.9 61.2 %copy-start.9 = (bf16[672,512]{1,0:T(8,128)(2,1)}, bf16[672,512]{1,0:T(8,128)(2,1)S(1)}, u32[]{:S(2)}) copy-start(bf16[672,512]{1,0:T(8,128)(2,1)S(1)} %collective-permute-done.7.refs_4_) | copy-start | bytes 2064388
  80.9 44.9 %collective-permute-start.14 = (bf16[336,1024]{1,0:T(8,128)(2,1)S(1)}, bf16[336,1024]{1,0:T(8,128)(2,1)}, u32[]{:S(2)}, u32[]{:S(2)}) collective-permute-start(bf16[336,1024]{1,0:T(8,128)(2,1)S(1)} %get-tuple-element.9), channel_id=1, source_target_pairs={{0,8},{4,12},{8,0},{12,4},{1,9},{5,13},{9,1},{13,5},{2,10},{6,14},... | collective-permute-start | bytes 2064392 | tf_op jit(solution)/shard_map/ppermute | solution.py:609
  82.3 61.4 %collective-permute-start.16 = (bf16[336,1024]{1,0:T(8,128)(2,1)}, bf16[336,1024]{1,0:T(8,128)(2,1)}, u32[]{:S(2)}, u32[]{:S(2)}) collective-permute-start(bf16[336,1024]{1,0:T(8,128)(2,1)} %get-tuple-element.8), channel_id=1, source_target_pairs={{0,8},{4,12},{8,0},{12,4},{1,9},{5,13},{9,1},{13,5},{2,10},{6,14},... | collective-permute-start | bytes 2064392 | tf_op jit(solution)/shard_map/ppermute | solution.py:609
  96.3 60.7 %collective-permute-start.6 = (bf16[1344,512]{1,0:T(8,128)(2,1)}, bf16[1344,512]{1,0:T(8,128)(2,1)}, u32[]{:S(2)}, u32[]{:S(2)}) collective-permute-start(bf16[1344,512]{1,0:T(8,128)(2,1)} %bitcast.50), channel_id=1, source_target_pairs={{0,4},{4,0},{8,12},{12,8},{1,5},{5,1},{9,13},{13,9},{2,6},{6,2},{1... | collective-permute-start | bytes 4128776 | tf_op jit(solution)/shard_map/ppermute | solution.py:595
  110.1 44.6 %collective-permute-start.8 = (bf16[672,512]{1,0:T(8,128)(2,1)S(1)}, bf16[672,512]{1,0:T(8,128)(2,1)}, u32[]{:S(2)}, u32[]{:S(2)}) collective-permute-start(bf16[672,512]{1,0:T(8,128)(2,1)S(1)} %collective-permute-done.7.refs_4_), channel_id=1, source_target_pairs={{0,16},{16,0},{1,17},{17,1},{2,18},{18,2},{3,19},{19,3},{4,20},{20... | collective-permute-start | bytes 2064392 | tf_op jit(solution)/shard_map/ppermute | solution.py:596
  125.8 29.4 %collective-permute-start.10 = (bf16[672,512]{1,0:T(8,128)(2,1)}, bf16[672,512]{1,0:T(8,128)(2,1)}, u32[]{:S(2)}, u32[]{:S(2)}) collective-permute-start(bf16[672,512]{1,0:T(8,128)(2,1)} %collective-permute-done.9.refs_6_), channel_id=1, source_target_pairs={{0,16},{16,0},{1,17},{17,1},{2,18},{18,2},{3,19},{19,3},{4,20},{20... | collective-permute-start | bytes 2064392 | tf_op jit(solution)/shard_map/ppermute | solution.py:597
  142.1 10.6 %copy-start.4 = (bf16[1344,1024]{1,0:T(8,128)(2,1)S(1)}, bf16[1344,1024]{1,0:T(8,128)(2,1)}, u32[]{:S(2)}) copy-start(bf16[1344,1024]{1,0:T(8,128)(2,1)} %param.14) | copy-start | bytes 8257540
  143.8 8.9 %collective-permute-start.23 = (bf16[1344,128]{1,0:T(8,128)(2,1)S(1)}, bf16[1344,128]{1,0:T(8,128)(2,1)S(1)}, u32[]{:S(2)}, u32[]{:S(2)}) collective-permute-start(bf16[1344,128]{1,0:T(8,128)(2,1)S(1)} %slice.35), channel_id=1, source_target_pairs={{0,8},{4,12},{8,0},{12,4},{1,9},{5,13},{9,1},{13,5},{2,10},{6,14},... | collective-permute-start | bytes 1032200 | tf_op jit(solution)/shard_map/ppermute | solution.py:656
  152.7 85.9 %collective-permute-start.13 = (bf16[1344,1024]{1,0:T(8,128)(2,1)S(1)}, bf16[1344,1024]{1,0:T(8,128)(2,1)}, u32[]{:S(2)}, u32[]{:S(2)}) collective-permute-start(bf16[1344,1024]{1,0:T(8,128)(2,1)S(1)} %bitcast.75), channel_id=1, source_target_pairs={{0,4},{4,0},{8,12},{12,8},{1,5},{5,1},{9,13},{13,9},{2,6},{6,2},{1... | collective-permute-start | bytes 8257544 | tf_op jit(solution)/shard_map/ppermute | solution.py:605
  154.7 35.6 %collective-permute-start.1 = (bf16[1344,512]{1,0:T(8,128)(2,1)}, bf16[1344,512]{1,0:T(8,128)(2,1)}, u32[]{:S(2)}, u32[]{:S(2)}) collective-permute-start(bf16[1344,512]{1,0:T(8,128)(2,1)} %get-tuple-element.14), channel_id=1, source_target_pairs={{0,4},{4,0},{8,12},{12,8},{1,5},{5,1},{9,13},{13,9},{2,6},{6,2},{1... | collective-permute-start | bytes 4128776 | tf_op jit(solution)/shard_map/ppermute | solution.py:595
  155.2 18.5 %collective-permute-start.3 = (bf16[672,512]{1,0:T(8,128)(2,1)}, bf16[672,512]{1,0:T(8,128)(2,1)S(1)}, u32[]{:S(2)}, u32[]{:S(2)}) collective-permute-start(bf16[672,512]{1,0:T(8,128)(2,1)} %collective-permute-done.2.refs_4_), channel_id=1, source_target_pairs={{0,16},{16,0},{1,17},{17,1},{2,18},{18,2},{3,19},{19,3},{4,20},{20... | collective-permute-start | bytes 2064392 | tf_op jit(solution)/shard_map/ppermute | solution.py:596
  156.8 184.4 %reduce-scatter.2.cloned.1.call-start = ((), (), s32[]{:S(2)}) async-start(), calls=%async_computation.1 | async-start | bytes 3440640 | tf_op jit(solution)/shard_map/reduce_scatter | solution.py:700
  157.0 31.6 %collective-permute-start.5 = (bf16[672,512]{1,0:T(8,128)(2,1)}, bf16[672,512]{1,0:T(8,128)(2,1)}, u32[]{:S(2)}, u32[]{:S(2)}) collective-permute-start(bf16[672,512]{1,0:T(8,128)(2,1)} %collective-permute-done.4.refs_6_), channel_id=1, source_target_pairs={{0,16},{16,0},{1,17},{17,1},{2,18},{18,2},{3,19},{19,3},{4,20},{20... | collective-permute-start | bytes 2064392 | tf_op jit(solution)/shard_map/ppermute | solution.py:597
  173.7 12.0 %copy-start.10 = (bf16[672,512]{1,0:T(8,128)(2,1)}, bf16[672,512]{1,0:T(8,128)(2,1)S(1)}, u32[]{:S(2)}) copy-start(bf16[672,512]{1,0:T(8,128)(2,1)S(1)} %collective-permute-done.3.refs_5_) | copy-start | bytes 2064388
  173.7 29.6 %collective-permute-start.15 = (bf16[336,1024]{1,0:T(8,128)(2,1)}, bf16[336,1024]{1,0:T(8,128)(2,1)}, u32[]{:S(2)}, u32[]{:S(2)}) collective-permute-start(bf16[336,1024]{1,0:T(8,128)(2,1)} %collective-permute-done.14.refs_2_), channel_id=1, source_target_pairs={{0,16},{16,0},{1,17},{17,1},{2,18},{18,2},{3,19},{19,3},{4,20},{20... | collective-permute-start | bytes 2064392 | tf_op jit(solution)/shard_map/ppermute | solution.py:610
  174.4 42.7 %collective-permute-start.17 = (bf16[336,1024]{1,0:T(8,128)(2,1)}, bf16[336,1024]{1,0:T(8,128)(2,1)}, u32[]{:S(2)}, u32[]{:S(2)}) collective-permute-start(bf16[336,1024]{1,0:T(8,128)(2,1)} %collective-permute-done.16.refs_4_), channel_id=1, source_target_pairs={{0,16},{16,0},{1,17},{17,1},{2,18},{18,2},{3,19},{19,3},{4,20},{20... | collective-permute-start | bytes 2064392 | tf_op jit(solution)/shard_map/ppermute | solution.py:610
  188.6 28.6 %collective-permute-start.11 = (bf16[512,512]{1,0:T(8,128)(2,1)}, bf16[512,512]{1,0:T(8,128)(2,1)S(1)}, u32[]{:S(2)}, u32[]{:S(2)}) collective-permute-start(bf16[512,512]{1,0:T(8,128)(2,1)} %project.5.k0.v0), channel_id=1, source_target_pairs={{0,8},{4,12},{8,0},{12,4},{1,9},{5,13},{9,1},{13,5},{2,10},{6,14},... | collective-permute-start | bytes 1572872 | tf_op jit(solution)/shard_map/ppermute | solution.py:686
  190.3 48.1 %collective-permute-start.18 = (bf16[336,1024]{1,0:T(8,128)(2,1)}, bf16[336,1024]{1,0:T(8,128)(2,1)}, u32[]{:S(2)}, u32[]{:S(2)}) collective-permute-start(bf16[336,1024]{1,0:T(8,128)(2,1)} %collective-permute-done.14.refs_2_), channel_id=1, source_target_pairs={{0,4},{4,0},{8,12},{12,8},{1,5},{5,1},{9,13},{13,9},{2,6},{6,2},{1... | collective-permute-start | bytes 2064392 | tf_op jit(solution)/shard_map/ppermute | solution.py:612
  203.3 35.3 %collective-permute-start.20 = (bf16[336,1024]{1,0:T(8,128)(2,1)}, bf16[336,1024]{1,0:T(8,128)(2,1)}, u32[]{:S(2)}, u32[]{:S(2)}) collective-permute-start(bf16[336,1024]{1,0:T(8,128)(2,1)} %collective-permute-done.16.refs_4_), channel_id=1, source_target_pairs={{0,4},{4,0},{8,12},{12,8},{1,5},{5,1},{9,13},{13,9},{2,6},{6,2},{1... | collective-permute-start | bytes 2064392 | tf_op jit(solution)/shard_map/ppermute | solution.py:612
  217.2 21.4 %collective-permute-start.19 = (bf16[336,1024]{1,0:T(8,128)(2,1)}, bf16[336,1024]{1,0:T(8,128)(2,1)}, u32[]{:S(2)}, u32[]{:S(2)}) collective-permute-start(bf16[336,1024]{1,0:T(8,128)(2,1)} %collective-permute-done.15.refs_3_), channel_id=1, source_target_pairs={{0,4},{4,0},{8,12},{12,8},{1,5},{5,1},{9,13},{13,9},{2,6},{6,2},{1... | collective-permute-start | bytes 2064392 | tf_op jit(solution)/shard_map/ppermute | solution.py:612
  217.2 9.2 %copy-start.3 = (bf16[512,512]{1,0:T(8,128)(2,1)}, bf16[512,512]{1,0:T(8,128)(2,1)S(1)}, u32[]{:S(2)}) copy-start(bf16[512,512]{1,0:T(8,128)(2,1)S(1)} %collective-permute-done.11.k2.v2) | copy-start | bytes 1572868
  217.2 21.4 %collective-permute-start.21 = (bf16[336,1024]{1,0:T(8,128)(2,1)}, bf16[336,1024]{1,0:T(8,128)(2,1)}, u32[]{:S(2)}, u32[]{:S(2)}) collective-permute-start(bf16[336,1024]{1,0:T(8,128)(2,1)} %collective-permute-done.17.refs_5_), channel_id=1, source_target_pairs={{0,4},{4,0},{8,12},{12,8},{1,5},{5,1},{9,13},{13,9},{2,6},{6,2},{1... | collective-permute-start | bytes 2064392 | tf_op jit(solution)/shard_map/ppermute | solution.py:612
  238.4 1.5 collective-permute-start.12
  239.9 0.7 copy-start.13
  254.7 3.4 collective-permute-start.24
  258.1 1.1 copy-start.5
  279.9 1.3 collective-permute-start.25
  281.2 0.7 copy-start.14
  291.5 15.6 %copy-start.2 = (bf16[4,1344,128]{2,1,0:T(8,128)(2,1)S(1)}, bf16[4,1344,128]{2,1,0:T(8,128)(2,1)}, u32[]{:S(2)}) copy-start(bf16[4,1344,128]{2,1,0:T(8,128)(2,1)} %project_out.3) | copy-start | bytes 4128772
  292.8 14.3 %collective-permute-start.26 = (bf16[1344,128]{1,0:T(8,128)(2,1)S(1)}, bf16[1344,128]{1,0:T(8,128)(2,1)S(1)}, u32[]{:S(2)}, u32[]{:S(2)}) collective-permute-start(bf16[1344,128]{1,0:T(8,128)(2,1)S(1)} %get-tuple-element.18), channel_id=1, source_target_pairs={{0,1},{4,5},{8,9},{12,13},{16,17},{20,21},{24,25},{28,29}} | collective-permute-start | bytes 1032200 | tf_op jit(solution)/shard_map/ppermute | solution.py:567
  294.4 17.3 %collective-permute-start.29 = (bf16[1344,128]{1,0:T(8,128)(2,1)S(1)}, bf16[1344,128]{1,0:T(8,128)(2,1)S(1)}, u32[]{:S(2)}, u32[]{:S(2)}) collective-permute-start(bf16[1344,128]{1,0:T(8,128)(2,1)S(1)} %get-tuple-element.19), channel_id=1, source_target_pairs={{3,2},{7,6},{11,10},{15,14},{19,18},{23,22},{27,26},{31,30}} | collective-permute-start | bytes 1032200 | tf_op jit(solution)/shard_map/ppermute | solution.py:568
  307.2 11.8 %collective-permute-start.27 = (bf16[1344,128]{1,0:T(8,128)(2,1)S(1)}, bf16[1344,128]{1,0:T(8,128)(2,1)S(1)}, u32[]{:S(2)}, u32[]{:S(2)}) collective-permute-start(bf16[1344,128]{1,0:T(8,128)(2,1)S(1)} %fusion.7), channel_id=1, source_target_pairs={{0,1},{1,2},{4,5},{5,6},{8,9},{9,10},{12,13},{13,14},{16,17},{17,1... | collective-permute-start | bytes 1032200 | tf_op jit(solution)/shard_map/ppermute | solution.py:567
  319.1 5.9 %collective-permute-start.30 = (bf16[1344,128]{1,0:T(8,128)(2,1)S(1)}, bf16[1344,128]{1,0:T(8,128)(2,1)S(1)}, u32[]{:S(2)}, u32[]{:S(2)}) collective-permute-start(bf16[1344,128]{1,0:T(8,128)(2,1)S(1)} %get-tuple-element.17), channel_id=1, source_target_pairs={{3,2},{2,1},{7,6},{6,5},{11,10},{10,9},{15,14},{14,13},{19,18},{18... | collective-permute-start | bytes 1032200 | tf_op jit(solution)/shard_map/ppermute | solution.py:568
  319.8 29.5 %copy-start.6 = (bf16[1344,128]{1,0:T(8,128)(2,1)S(1)}, bf16[1344,128]{1,0:T(8,128)(2,1)}, u32[]{:S(2)}) copy-start(bf16[1344,128]{1,0:T(8,128)(2,1)} %multiply_convert_fusion) | copy-start | bytes 1032196
  319.8 11.7 %collective-permute-start.28 = (bf16[1344,128]{1,0:T(8,128)(2,1)S(1)}, bf16[1344,128]{1,0:T(8,128)(2,1)S(1)}, u32[]{:S(2)}, u32[]{:S(2)}) collective-permute-start(bf16[1344,128]{1,0:T(8,128)(2,1)S(1)} %get-tuple-element.16), channel_id=1, source_target_pairs={{0,1},{1,2},{2,3},{4,5},{5,6},{6,7},{8,9},{9,10},{10,11},{12,13},{... | collective-permute-start | bytes 1032200 | tf_op jit(solution)/shard_map/ppermute | solution.py:567
  325.1 15.8 %collective-permute-start.31 = (bf16[1344,128]{1,0:T(8,128)(2,1)S(1)}, bf16[1344,128]{1,0:T(8,128)(2,1)S(1)}, u32[]{:S(2)}, u32[]{:S(2)}) collective-permute-start(bf16[1344,128]{1,0:T(8,128)(2,1)S(1)} %fusion.6), channel_id=1, source_target_pairs={{3,2},{2,1},{1,0},{7,6},{6,5},{5,4},{11,10},{10,9},{9,8},{15,14},{... | collective-permute-start | bytes 1032200 | tf_op jit(solution)/shard_map/ppermute | solution.py:568
  340.9 0.7 copy-start.11
  343.0 10.3 %copy-start.7 = (bf16[256,1344]{0,1:T(8,128)(2,1)S(1)}, bf16[256,1344]{0,1:T(8,128)(2,1)}, u32[]{:S(2)}) copy-start(bf16[256,1344]{0,1:T(8,128)(2,1)} %param.10) | copy-start | bytes 2064388
  343.0 10.3 %copy-start.8 = (bf16[1,1344,256]{2,1,0:T(8,128)(2,1)S(1)}, bf16[1,1344,256]{2,1,0:T(8,128)(2,1)}, u32[]{:S(2)}) copy-start(bf16[1,1344,256]{2,1,0:T(8,128)(2,1)} %reduce-scatter.2.cloned.1.call-done) | copy-start | bytes 2064388
  343.0 5.8 %collective-permute-start.32 = (f32[1,384]{1,0:T(1,128)S(1)}, f32[1,384]{1,0:T(1,128)S(1)}, u32[]{:S(2)}, u32[]{:S(2)}) collective-permute-start(f32[1,384]{1,0:T(1,128)S(1)} %pad_maximum_fusion), channel_id=1, source_target_pairs={{0,1},{1,2},{2,3},{3,0},{4,5},{5,6},{6,7},{7,4},{8,9},{9,10},{10,1... | collective-permute-start | bytes 4616 | tf_op jit(solution)/shard_map/ppermute | solution.py:579
  344.8 4.5 %collective-permute-start.33 = (f32[1,384]{1,0:T(1,128)S(1)}, f32[1,384]{1,0:T(1,128)S(1)}, u32[]{:S(2)}, u32[]{:S(2)}) collective-permute-start(f32[1,384]{1,0:T(1,128)S(1)} %pad_maximum_fusion), channel_id=1, source_target_pairs={{0,2},{1,3},{2,0},{3,1},{4,6},{5,7},{6,4},{7,5},{8,10},{9,11},{10,... | collective-permute-start | bytes 4616 | tf_op jit(solution)/shard_map/ppermute | solution.py:579
  345.2 4.2 %collective-permute-start.34 = (f32[1,384]{1,0:T(1,128)S(1)}, f32[1,384]{1,0:T(1,128)S(1)}, u32[]{:S(2)}, u32[]{:S(2)}) collective-permute-start(f32[1,384]{1,0:T(1,128)S(1)} %pad_maximum_fusion), channel_id=1, source_target_pairs={{0,3},{1,0},{2,1},{3,2},{4,7},{5,4},{6,5},{7,6},{8,11},{9,8},{10,9... | collective-permute-start | bytes 4616 | tf_op jit(solution)/shard_map/ppermute | solution.py:579
Sparse Core Ops, SparseCore 0:
  9.5 59.6 all-gather.4
  156.9 32.4 all-gather.6
  251.0 55.6 reduce-scatter.1

commit v2 on v1

--- a/solution.py
+++ b/solution.py
@@ -204,6 +204,7 @@
             )
 
     acc[...] = jnp.zeros_like(acc)
+    held[...] = jnp.zeros_like(held)
 
     @pl.when(rounds > 0)
     def _():
@@ -226,15 +227,13 @@
         at = lax.broadcasted_iota(jnp.int32, lane.shape, 1) - within * BATCH
         rel = jnp.where((lane >= 0) & (at >= 0) & (at < BATCH), at * 128 + lane, -1)
         hot = lax.broadcasted_iota(jnp.int32, (width, 128), 0) == rel
-        got = jnp.dot(buf[slot], hot.astype(jnp.bfloat16), preferred_element_type=jnp.float32)
-
-        @pl.when(within == 0)
-        def _():
-            held[...] = got
-
-        @pl.when(within > 0)
-        def _():
-            held[...] += got
+        hot = hot.astype(jnp.bfloat16)
+        size = held.shape[0] // 4
+        keep = jnp.where(within == 0, 0.0, 1.0)
+        for start in range(0, held.shape[0], size):
+            span = pl.ds(start, size)
+            got = jnp.dot(buf[slot, span, :], hot, preferred_element_type=jnp.float32)
+            held[span, :] = held[span, :] * keep + got
 
         @pl.when((within == per_group - 1) | (step == rounds - 1))
         def _():
@@ -566,6 +565,7 @@
             send_b = (send_b.astype(jnp.float32) + b.astype(jnp.float32)).astype(jnp.bfloat16)
         a = lax.ppermute(send_a, axis, [(i, i + 1) for i in range(step)])
         b = lax.ppermute(send_b, axis, [(count - 1 - i, count - 2 - i) for i in range(step)])
+        a, b = lax.optimization_barrier((a, b))
     return (
         block(index).astype(jnp.float32) + a.astype(jnp.float32) + b.astype(jnp.float32)
     )
@@ -653,7 +653,8 @@
         held.append(pick_rows(embed.T, jnp.concatenate(wanted), start))
     give, keep = held
     keep = keep + lax.ppermute(give, "seq", swap(1))
-    mine = keep[:, :cont_rows] + lax.ppermute(keep[:, cont_rows:], "seq", swap(2))
+    theirs = lax.ppermute(keep[:, cont_rows:], "seq", swap(2))
+    mine = keep[:, :cont_rows] + theirs
     cont_t = (mine.astype(jnp.float32) * math.sqrt(full_width)).astype(jnp.bfloat16)
     cont_x = lax.all_gather(cont_t, "tp", axis=0)
 

time: 362 us -> 359 us (level)
  waiting for transfers between devices: 156 us -> 151 us
    ppermute x3, waiting for transfers between devices: 9.46 us -> 4.14 us  [line_scatter(): lax.ppermute(send_b, axis, [(count - 1 - i, count - 2 - i) for i in range...]
    ppermute x3, starting transfers between devices: 11.1 us -> 14.8 us  [line_scatter(): a = lax.ppermute(send_a, axis, [(i, i + 1) for i in range(step)])]
  transfers between devices with their start and end apart: 38 -> 38, of which waited for: 17 -> 18; matrix products, arithmetic and copies ran while one was open for 10% -> 10% of each run, Pallas kernels for 28% -> 28%
where the time goes in v2:
time: 359 us; the launch traced here: 358 us
  waiting for transfers between devices  151 us (42%)
  Pallas kernels  99.9 us (28%)
  starting transfers between devices  46.8 us (13%)
  local copies, waits for them, and re-layouts  28.5 us (8%)
  other arithmetic  17.5 us (5%)
  between operations  14.1 us (4%)
    pallas_call x4, Pallas kernels, project(): pl.pallas_call(functools.partial(proj_kernel, normed_cols, len(sources),...  28.9 us
    ppermute x2, waiting for transfers between devices, full_pieces(): more = lax.ppermute(got, 'grp', ACROSS)  26.8 us
    pallas_call x2, Pallas kernels, pick_rows(): pl.pallas_call(pick_kernel, out_shape=jax.ShapeDtypeStruct((width, rows),...  25.3 us
    ppermute x3, waiting for transfers between devices, line_scatter(): a = lax.ppermute(send_a, axis, [(i, i + 1) for i in range(step)])  23.6 us
    all_gather x1, waiting for transfers between devices, paired_device(): prompt_x = lax.all_gather(prompt_t, 'tp', axis=0)  23.1 us
    pallas_call x2, Pallas kernels, project_out(): pl.pallas_call(functools.partial(out_kernel, len(near)), out_shape=jax.Sh...  19.7 us
    pallas_call x2, Pallas kernels, attend_rows(): pl.pallas_call(kernel, out_shape=jax.ShapeDtypeStruct((2, rows, q_cols),...  17.1 us
    ppermute x2, waiting for transfers between devices, half_pieces(): near_x = lax.ppermute(near, 'grp', ACROSS)  15.3 us
  transfers between devices with their start and end apart: 38, of which 18 were waited for; matrix products, arithmetic and copies ran while one was open for 10% of the time, Pallas kernels for 28%

profile of v2, /device:TPU:0, one launch (start us, length us, event | category | flops | bytes accessed | tf_op | source)
XLA Modules:
  0.0 357.9 jit_solution(6156086708981305014)
XLA Ops:
  9.8 0.8 copy.17.listed
  13.3 1.9 pad_add_fusion
  15.2 12.1 %pick_rows.3 = bf16[1344,256]{1,0:T(8,128)(2,1)} custom-call(s32[265]{0:T(512)} %get-tuple-element.50.info, bf16[1344,32768]{1,0:T(8,128)(2,1)} %bitcast.18.emb, s32[2,128]{1,0:T(2,128)} %get-tuple-element.46.lanes, s32[256,1]{1,0:T(8,128)} %copy.17.listed, s32[1,256]{1,0:T(1,128)} %and_select_fusion.ids), custom_call_target="tpu_custom_call" | custom-call | tf_op jit(solution)/shard_map/pick_rows/pallas_call | solution.py:272
  27.2 2.3 collective-permute-start.22
  29.5 3.6 %constant_dynamic-slice_fusion.6 = (bf16[1344,2,256]{2,1,0:T(2,128)(2,1)S(1)}, bf16[1344,2,256]{2,1,0:T(2,128)(2,1)S(1)}) fusion(bf16[1344,2,512]{2,1,0:T(2,128)(2,1)} %param.15, s32[]{:T(128)S(6)} %select_n.206, s32[]{:T(128)S(6)} %select_n.205), kind=kLoop, calls=%fused_computation.57 | loop fusion | bytes 5505032 | tf_op jit(solution)/shard_map/dynamic_slice | solution.py:641
  33.5 1.0 constant_dynamic-slice_fusion.5
  34.5 6.8 %collective-permute-start.7 = (bf16[672,512]{1,0:T(8,128)(2,1)}, bf16[672,512]{1,0:T(8,128)(2,1)S(1)}, u32[]{:S(2)}, u32[]{:S(2)}) collective-permute-start(bf16[672,512]{1,0:T(8,128)(2,1)} %constant_dynamic-slice_fusion.5), channel_id=1, source_target_pairs={{0,8},{4,12},{8,0},{12,4},{1,9},{5,13},{9,1},{13,5},{2,10},{6,14},... | collective-permute-start | bytes 2064392 | tf_op jit(solution)/shard_map/ppermute | solution.py:593
  41.2 1.4 copy.20
  42.7 2.0 constant_dynamic-slice_fusion.4
  46.1 23.1 %all-gather.5.cloned.1.call-done = bf16[5376,256]{1,0:T(8,128)(2,1)} async-done(((bf16[1344,256]{1,0:T(8,128)(2,1)}), bf16[5376,256]{1,0:T(8,128)(2,1)}) %all-gather.5.cloned.1.call-update) | async-done | bytes 2752528 | tf_op jit(solution)/shard_map/all_gather | solution.py:637
  69.2 5.1 %norm_rows.2.refs_0_ = bf16[256,5632]{1,0:T(8,128)(2,1)} custom-call(s32[3]{0:T(128)} %pad_add_fusion.2.pos, f32[4,1344]{1,0:T(4,128)} %reshape.287.gain, bf16[4,1344,256]{2,1,0:T(8,128)(2,1)} %bitcast.81), custom_call_target="tpu_custom_call" | custom-call | tf_op jit(solution)/shard_map/norm_rows/pallas_call | solution.py:315
  74.3 3.4 fusion.35
  77.7 1.5 collective-permute-start.2
  79.2 0.9 dynamic-slice_bitcast_fusion
  80.9 1.5 collective-permute-start.14
  82.9 13.4 %collective-permute-done.2.refs_4_ = bf16[672,512]{1,0:T(8,128)(2,1)} collective-permute-done((bf16[672,512]{1,0:T(8,128)(2,1)}, bf16[672,512]{1,0:T(8,128)(2,1)}, u32[]{:S(2)}, u32[]{:S(2)}) %collective-permute-start.2) | collective-permute-done | bytes 688160 | tf_op jit(solution)/shard_map/ppermute | solution.py:593
  96.3 13.8 %collective-permute-done.4.refs_6_ = bf16[672,512]{1,0:T(8,128)(2,1)} collective-permute-done((bf16[672,512]{1,0:T(8,128)(2,1)S(1)}, bf16[672,512]{1,0:T(8,128)(2,1)}, u32[]{:S(2)}, u32[]{:S(2)}) %collective-permute-start.4) | collective-permute-done | bytes 688160 | tf_op jit(solution)/shard_map/ppermute | solution.py:594
  110.1 1.5 collective-permute-start.8
  111.6 14.2 %collective-permute-done.14.refs_2_ = bf16[336,1024]{1,0:T(8,128)(2,1)} collective-permute-done((bf16[336,1024]{1,0:T(8,128)(2,1)S(1)}, bf16[336,1024]{1,0:T(8,128)(2,1)}, u32[]{:S(2)}, u32[]{:S(2)}) %collective-permute-start.14) | collective-permute-done | bytes 688160 | tf_op jit(solution)/shard_map/ppermute | solution.py:609
  125.8 1.5 collective-permute-start.10
  128.7 13.2 %pick_rows.2 = bf16[1344,256]{1,0:T(8,128)(2,1)} custom-call(s32[265]{0:T(512)} %get-tuple-element.51.info, bf16[1344,32768]{1,0:T(8,128)(2,1)} %bitcast.18.emb, s32[2,128]{1,0:T(2,128)} %get-tuple-element.48.lanes, s32[256,1]{1,0:T(8,128)} %copy.16.listed, s32[1,256]{1,0:T(1,128)} %and_select_fusion.1.ids), custom_call_target="tpu_custom_call" | custom-call | tf_op jit(solution)/shard_map/pick_rows/pallas_call | solution.py:272
  141.9 1.6 add.200
  143.6 1.7 collective-permute-start.23
  145.2 7.2 %collective-permute-done.23 = bf16[1344,128]{1,0:T(8,128)(2,1)S(1)} collective-permute-done((bf16[1344,128]{1,0:T(8,128)(2,1)S(1)}, bf16[1344,128]{1,0:T(8,128)(2,1)S(1)}, u32[]{:S(2)}, u32[]{:S(2)}) %collective-permute-start.23) | collective-permute-done | bytes 344096 | tf_op jit(solution)/shard_map/ppermute | solution.py:656
  152.5 2.0 constant_dynamic-slice_fusion.8
  155.7 0.8 multiply_convert_fusion
  156.8 1.4 collective-permute-start.5
  158.2 15.3 %collective-permute-done.3.refs_5_ = bf16[672,512]{1,0:T(8,128)(2,1)S(1)} collective-permute-done((bf16[672,512]{1,0:T(8,128)(2,1)}, bf16[672,512]{1,0:T(8,128)(2,1)S(1)}, u32[]{:S(2)}, u32[]{:S(2)}) %collective-permute-start.3) | collective-permute-done | bytes 688160 | tf_op jit(solution)/shard_map/ppermute | solution.py:596
  174.2 1.3 collective-permute-start.17
  175.5 1.8 fusion.11
  177.4 8.1 %project.5.k0.v0 = bf16[512,512]{1,0:T(8,128)(2,1)} custom-call(s32[3]{0:T(128)} %pad_add_fusion.2.pos, f32[1,128]{1,0:T(1,128)} %bitcast.96, f32[512,128]{1,0:T(8,128)} %get-tuple-element.39.cosine, f32[512,128]{1,0:T(8,128)} %get-tuple-element.38.sine, bf16[256,5632]{1,0:T(8,128)(2,1)} %norm_rows.2.refs_0_, ...), custom_call_target="tpu_custom_call" | custom-call | tf_op jit(solution)/shard_map/project/pallas_call | solution.py:390
  185.5 2.9 collective-permute-done.5.refs_7_
  188.4 1.7 collective-permute-start.11
  190.1 13.0 %collective-permute-done.15.refs_3_ = bf16[336,1024]{1,0:T(8,128)(2,1)} collective-permute-done((bf16[336,1024]{1,0:T(8,128)(2,1)}, bf16[336,1024]{1,0:T(8,128)(2,1)}, u32[]{:S(2)}, u32[]{:S(2)}) %collective-permute-start.15) | collective-permute-done | bytes 688160 | tf_op jit(solution)/shard_map/ppermute | solution.py:610
  203.1 13.8 %collective-permute-done.17.refs_5_ = bf16[336,1024]{1,0:T(8,128)(2,1)} collective-permute-done((bf16[336,1024]{1,0:T(8,128)(2,1)}, bf16[336,1024]{1,0:T(8,128)(2,1)}, u32[]{:S(2)}, u32[]{:S(2)}) %collective-permute-start.17) | collective-permute-done | bytes 688160 | tf_op jit(solution)/shard_map/ppermute | solution.py:610
  217.5 8.7 %project.4.q = bf16[512,512]{1,0:T(8,128)(2,1)} custom-call(s32[3]{0:T(128)} %pad_add_fusion.2.pos, f32[1,128]{1,0:T(1,128)} %bitcast.98, f32[512,128]{1,0:T(8,128)} %get-tuple-element.39.cosine, f32[512,128]{1,0:T(8,128)} %get-tuple-element.38.sine, bf16[256,5632]{1,0:T(8,128)(2,1)} %norm_rows.2.refs_0_, bf16[256,5632]{1,0:T(8,128)(2,1)} %collective-permute-done.refs_1_, ...), custom_call_target="tpu_custom_call" | custom-call | tf_op jit(solution)/shard_map/project/pallas_call | solution.py:390
  226.2 10.3 %attend_rows.2 = bf16[2,256,512]{2,1,0:T(8,128)(2,1)} custom-call(s32[3]{0:T(128)} %pad_add_fusion.2.pos, bf16[512,512]{1,0:T(8,128)(2,1)} %project.4.q, bf16[512,512]{1,0:T(8,128)(2,1)} %project.5.k0.v0, bf16[512,512]{1,0:T(8,128)(2,1)} %copy-done.3, bf16[512,512]{1,0:T(8,128)(2,1)} %project.5.k0.v0, bf16[512,512]{1,0:T(8,128)(2,1)} %copy-done.3), custom_call_target="tpu_custom_call" | custom-call | tf_op jit(solution)/shard_map/attend_rows/pallas_call | solution.py:490
  236.4 1.8 slice_bitcast_fusion
  238.4 1.3 collective-permute-done.12.theirs
  240.4 10.1 %project_out.2 = bf16[4,1344,256]{2,1,0:T(8,128)(2,1)} custom-call(s32[3]{0:T(128)} %pad_add_fusion.2.pos, bf16[256,512]{1,0:T(8,128)(2,1)} %get-tuple-element.35.mine, bf16[256,512]{1,0:T(8,128)(2,1)} %copy-done.13, bf16[1344,1024]{1,0:T(8,128)(2,1)} %bitcast.73, bf16[1344,1024]{1,0:T(8,128)(2,1)} %collective-permute-done.13.refs_1_, ...), custom_call_target="tpu_custom_call" | custom-call | tf_op jit(solution)/shard_map/project_out/pallas_call | solution.py:536
  250.6 3.8 %norm_rows.3.refs_0_ = bf16[128,5632]{1,0:T(8,128)(2,1)} custom-call(s32[3]{0:T(128)} %pad_add_fusion.2.pos, f32[4,1344]{1,0:T(4,128)} %reshape.287.gain, bf16[4,1344,128]{2,1,0:T(8,128)(2,1)} %bitcast.83), custom_call_target="tpu_custom_call" | custom-call | tf_op jit(solution)/shard_map/norm_rows/pallas_call | solution.py:315
  254.7 1.2 fusion.20
  255.9 2.0 collective-permute-done.24.refs_1_
  257.9 1.1 copy-done.5
  259.0 6.0 %project.7.ck.cv = bf16[256,512]{1,0:T(8,128)(2,1)} custom-call(s32[3]{0:T(128)} %pad_add_fusion.2.pos, f32[1,128]{1,0:T(1,128)} %bitcast.97, f32[256,128]{1,0:T(8,128)} %get-tuple-element.45.cosine, f32[256,128]{1,0:T(8,128)} %get-tuple-element.44.sine, bf16[128,5632]{1,0:T(8,128)(2,1)} %norm_rows.3.refs_0_, bf16[128,5632]{1,0:T(8,128)(2,1)} %copy-done.5, ...), custom_call_target="tpu_custom_call" | custom-call | tf_op jit(solution)/shard_map/project/pallas_call | solution.py:390
  265.0 6.1 %project.6.q = bf16[256,512]{1,0:T(8,128)(2,1)} custom-call(s32[3]{0:T(128)} %pad_add_fusion.2.pos, f32[1,128]{1,0:T(1,128)} %bitcast.99, f32[256,128]{1,0:T(8,128)} %get-tuple-element.45.cosine, f32[256,128]{1,0:T(8,128)} %get-tuple-element.44.sine, bf16[128,5632]{1,0:T(8,128)(2,1)} %norm_rows.3.refs_0_, bf16[128,5632]{1,0:T(8,128)(2,1)} %copy-done.5, ...), custom_call_target="tpu_custom_call" | custom-call | tf_op jit(solution)/shard_map/project/pallas_call | solution.py:390
  271.1 6.9 %attend_rows.3 = bf16[2,128,512]{2,1,0:T(8,128)(2,1)} custom-call(s32[3]{0:T(128)} %pad_add_fusion.2.pos, bf16[256,512]{1,0:T(8,128)(2,1)} %project.6.q, bf16[512,512]{1,0:T(8,128)(2,1)} %project.5.k0.v0, bf16[512,512]{1,0:T(8,128)(2,1)} %copy-done.3, bf16[512,512]{1,0:T(8,128)(2,1)} %project.5.k0.v0, bf16[512,512]{1,0:T(8,128)(2,1)} %copy-done.3, ...), custom_call_target="tpu_custom_call" | custom-call | tf_op jit(solution)/shard_map/attend_rows/pallas_call | solution.py:490
  278.0 1.6 slice_bitcast_fusion.2
  279.8 1.1 collective-permute-done.25.theirs
  281.6 9.6 %project_out.3 = bf16[4,1344,128]{2,1,0:T(8,128)(2,1)} custom-call(s32[3]{0:T(128)} %pad_add_fusion.2.pos, bf16[128,512]{1,0:T(8,128)(2,1)} %get-tuple-element.37.mine, bf16[128,512]{1,0:T(8,128)(2,1)} %copy-done.14, bf16[1344,1024]{1,0:T(8,128)(2,1)} %bitcast.74, bf16[1344,1024]{1,0:T(8,128)(2,1)} %collective-permute-done.13.refs_1_, ...), custom_call_target="tpu_custom_call" | custom-call | tf_op jit(solution)/shard_map/project_out/pallas_call | solution.py:536
  291.3 1.3 dynamic-slice_bitcast_fusion.2
  292.5 1.6 collective-permute-start.26
  294.8 12.0 %collective-permute-done.26 = bf16[1344,128]{1,0:T(8,128)(2,1)S(1)} collective-permute-done((bf16[1344,128]{1,0:T(8,128)(2,1)S(1)}, bf16[1344,128]{1,0:T(8,128)(2,1)S(1)}, u32[]{:S(2)}, u32[]{:S(2)}) %collective-permute-start.26) | collective-permute-done | bytes 344096 | tf_op jit(solution)/shard_map/ppermute | solution.py:566
  307.0 4.4 %collective-permute-start.28 = (bf16[1344,128]{1,0:T(8,128)(2,1)S(1)}, bf16[1344,128]{1,0:T(8,128)(2,1)S(1)}, u32[]{:S(2)}, u32[]{:S(2)}) collective-permute-start(bf16[1344,128]{1,0:T(8,128)(2,1)S(1)} %get-tuple-element.31), channel_id=1, source_target_pairs={{0,1},{1,2},{4,5},{5,6},{8,9},{9,10},{12,13},{13,14},{16,17},{17,1... | collective-permute-start | bytes 1032200 | tf_op jit(solution)/shard_map/ppermute | solution.py:566
  312.1 6.7 %collective-permute-done.28 = bf16[1344,128]{1,0:T(8,128)(2,1)S(1)} collective-permute-done((bf16[1344,128]{1,0:T(8,128)(2,1)S(1)}, bf16[1344,128]{1,0:T(8,128)(2,1)S(1)}, u32[]{:S(2)}, u32[]{:S(2)}) %collective-permute-start.28) | collective-permute-done | bytes 344096 | tf_op jit(solution)/shard_map/ppermute | solution.py:566
  319.0 8.8 %collective-permute-start.30 = (bf16[1344,128]{1,0:T(8,128)(2,1)S(1)}, bf16[1344,128]{1,0:T(8,128)(2,1)S(1)}, u32[]{:S(2)}, u32[]{:S(2)}) collective-permute-start(bf16[1344,128]{1,0:T(8,128)(2,1)S(1)} %get-tuple-element.29), channel_id=1, source_target_pairs={{0,1},{1,2},{2,3},{4,5},{5,6},{6,7},{8,9},{9,10},{10,11},{12,13},{... | collective-permute-start | bytes 1032200 | tf_op jit(solution)/shard_map/ppermute | solution.py:566
  327.8 1.3 collective-permute-start.31
  329.1 4.9 %collective-permute-done.30 = bf16[1344,128]{1,0:T(8,128)(2,1)S(1)} collective-permute-done((bf16[1344,128]{1,0:T(8,128)(2,1)S(1)}, bf16[1344,128]{1,0:T(8,128)(2,1)S(1)}, u32[]{:S(2)}, u32[]{:S(2)}) %collective-permute-start.30) | collective-permute-done | bytes 344096 | tf_op jit(solution)/shard_map/ppermute | solution.py:566
  334.0 4.1 %collective-permute-done.31 = bf16[1344,128]{1,0:T(8,128)(2,1)S(1)} collective-permute-done((bf16[1344,128]{1,0:T(8,128)(2,1)S(1)}, bf16[1344,128]{1,0:T(8,128)(2,1)S(1)}, u32[]{:S(2)}, u32[]{:S(2)}) %collective-permute-start.31) | collective-permute-done | bytes 344096 | tf_op jit(solution)/shard_map/ppermute | solution.py:567
  338.9 1.3 fusion
  340.6 3.5 collective-permute-start.34
  346.3 2.0 fusion.10
  348.3 1.9 copy.18
  350.2 1.2 fusion.4
  (111 shorter events, 19.4 us)
Async XLA Ops:
  7.2 62.1 %all-gather.5.cloned.1.call-start = ((), (), s32[]{:S(2)}) async-start(), calls=%async_computation.2 | async-start | bytes 3440640 | tf_op jit(solution)/shard_map/all_gather | solution.py:637
  7.9 242.7 %all-gather.7.cloned.1.call-start = ((), (), s32[]{:S(2)}) async-start(), calls=%async_computation.3 | async-start | bytes 1720320 | tf_op jit(solution)/shard_map/all_gather | solution.py:659
  27.2 52.9 %collective-permute-start.22 = (bf16[1344,256]{1,0:T(8,128)(2,1)}, bf16[1344,256]{1,0:T(8,128)(2,1)}, u32[]{:S(2)}, u32[]{:S(2)}) collective-permute-start(bf16[1344,256]{1,0:T(8,128)(2,1)} %pick_rows.3), channel_id=1, source_target_pairs={{0,4},{4,0},{8,12},{12,8},{1,5},{5,1},{9,13},{13,9},{2,6},{6,2},{1... | collective-permute-start | bytes 2064392 | tf_op jit(solution)/shard_map/ppermute | solution.py:655
  33.5 9.2 %copy-start.1 = (bf16[168,8,2,256]{3,1,2,0:T(8,128)(2,1)}, bf16[168,8,2,256]{3,1,2,0:T(8,128)(2,1)S(1)}, u32[]{:S(2)}) copy-start(bf16[168,8,2,256]{3,1,2,0:T(8,128)(2,1)S(1)} %copy.19) | copy-start | bytes 4128772
  34.5 46.4 %collective-permute-start.7 = (bf16[672,512]{1,0:T(8,128)(2,1)}, bf16[672,512]{1,0:T(8,128)(2,1)S(1)}, u32[]{:S(2)}, u32[]{:S(2)}) collective-permute-start(bf16[672,512]{1,0:T(8,128)(2,1)} %constant_dynamic-slice_fusion.5), channel_id=1, source_target_pairs={{0,8},{4,12},{8,0},{12,4},{1,9},{5,13},{9,1},{13,5},{2,10},{6,14},... | collective-permute-start | bytes 2064392 | tf_op jit(solution)/shard_map/ppermute | solution.py:593
  42.7 2.1 copy-start.15
  44.7 37.7 %collective-permute-start.9 = (bf16[672,512]{1,0:T(8,128)(2,1)}, bf16[672,512]{1,0:T(8,128)(2,1)}, u32[]{:S(2)}, u32[]{:S(2)}) collective-permute-start(bf16[672,512]{1,0:T(8,128)(2,1)} %constant_dynamic-slice_fusion.4), channel_id=1, source_target_pairs={{0,12},{4,8},{8,4},{12,0},{1,13},{5,9},{9,5},{13,1},{2,14},{6,10},... | collective-permute-start | bytes 2064392 | tf_op jit(solution)/shard_map/ppermute | solution.py:594
  74.3 99.9 %collective-permute-start = (bf16[256,5632]{1,0:T(8,128)(2,1)}, bf16[256,5632]{1,0:T(8,128)(2,1)}, u32[]{:S(2)}, u32[]{:S(2)}) collective-permute-start(bf16[256,5632]{1,0:T(8,128)(2,1)} %norm_rows.2.refs_0_), channel_id=1, source_target_pairs={{0,4},{4,0},{8,12},{12,8},{1,5},{5,1},{9,13},{13,9},{2,6},{6,2},{1... | collective-permute-start | bytes 8650760 | tf_op jit(solution)/shard_map/ppermute | solution.py:680
  74.3 4.8 %copy-start = (bf16[1024,1344]{0,1:T(8,128)(2,1)S(1)}, bf16[1024,1344]{0,1:T(8,128)(2,1)}, u32[]{:S(2)}) copy-start(bf16[1024,1344]{0,1:T(8,128)(2,1)} %param.18) | copy-start | bytes 8257540
  77.7 18.6 %collective-permute-start.2 = (bf16[672,512]{1,0:T(8,128)(2,1)}, bf16[672,512]{1,0:T(8,128)(2,1)}, u32[]{:S(2)}, u32[]{:S(2)}) collective-permute-start(bf16[672,512]{1,0:T(8,128)(2,1)} %get-tuple-element.25), channel_id=1, source_target_pairs={{0,8},{4,12},{8,0},{12,4},{1,9},{5,13},{9,1},{13,5},{2,10},{6,14},... | collective-permute-start | bytes 2064392 | tf_op jit(solution)/shard_map/ppermute | solution.py:593
  79.2 1.3 copy-start.12
  80.5 29.6 %collective-permute-start.4 = (bf16[672,512]{1,0:T(8,128)(2,1)S(1)}, bf16[672,512]{1,0:T(8,128)(2,1)}, u32[]{:S(2)}, u32[]{:S(2)}) collective-permute-start(bf16[672,512]{1,0:T(8,128)(2,1)S(1)} %copy-done.12), channel_id=1, source_target_pairs={{0,12},{4,8},{8,4},{12,0},{1,13},{5,9},{9,5},{13,1},{2,14},{6,10},... | collective-permute-start | bytes 2064392 | tf_op jit(solution)/shard_map/ppermute | solution.py:594
  80.9 61.0 %copy-start.9 = (bf16[672,512]{1,0:T(8,128)(2,1)}, bf16[672,512]{1,0:T(8,128)(2,1)S(1)}, u32[]{:S(2)}) copy-start(bf16[672,512]{1,0:T(8,128)(2,1)S(1)} %collective-permute-done.7.refs_4_) | copy-start | bytes 2064388
  80.9 44.9 %collective-permute-start.14 = (bf16[336,1024]{1,0:T(8,128)(2,1)S(1)}, bf16[336,1024]{1,0:T(8,128)(2,1)}, u32[]{:S(2)}, u32[]{:S(2)}) collective-permute-start(bf16[336,1024]{1,0:T(8,128)(2,1)S(1)} %get-tuple-element.21), channel_id=1, source_target_pairs={{0,8},{4,12},{8,0},{12,4},{1,9},{5,13},{9,1},{13,5},{2,10},{6,14},... | collective-permute-start | bytes 2064392 | tf_op jit(solution)/shard_map/ppermute | solution.py:609
  82.3 61.2 %collective-permute-start.16 = (bf16[336,1024]{1,0:T(8,128)(2,1)}, bf16[336,1024]{1,0:T(8,128)(2,1)}, u32[]{:S(2)}, u32[]{:S(2)}) collective-permute-start(bf16[336,1024]{1,0:T(8,128)(2,1)} %get-tuple-element.20), channel_id=1, source_target_pairs={{0,8},{4,12},{8,0},{12,4},{1,9},{5,13},{9,1},{13,5},{2,10},{6,14},... | collective-permute-start | bytes 2064392 | tf_op jit(solution)/shard_map/ppermute | solution.py:609
  96.3 60.5 %collective-permute-start.6 = (bf16[1344,512]{1,0:T(8,128)(2,1)}, bf16[1344,512]{1,0:T(8,128)(2,1)}, u32[]{:S(2)}, u32[]{:S(2)}) collective-permute-start(bf16[1344,512]{1,0:T(8,128)(2,1)} %bitcast.50), channel_id=1, source_target_pairs={{0,4},{4,0},{8,12},{12,8},{1,5},{5,1},{9,13},{13,9},{2,6},{6,2},{1... | collective-permute-start | bytes 4128776 | tf_op jit(solution)/shard_map/ppermute | solution.py:595
  110.1 44.4 %collective-permute-start.8 = (bf16[672,512]{1,0:T(8,128)(2,1)S(1)}, bf16[672,512]{1,0:T(8,128)(2,1)}, u32[]{:S(2)}, u32[]{:S(2)}) collective-permute-start(bf16[672,512]{1,0:T(8,128)(2,1)S(1)} %collective-permute-done.7.refs_4_), channel_id=1, source_target_pairs={{0,16},{16,0},{1,17},{17,1},{2,18},{18,2},{3,19},{19,3},{4,20},{20... | collective-permute-start | bytes 2064392 | tf_op jit(solution)/shard_map/ppermute | solution.py:596
  125.8 29.2 %collective-permute-start.10 = (bf16[672,512]{1,0:T(8,128)(2,1)}, bf16[672,512]{1,0:T(8,128)(2,1)}, u32[]{:S(2)}, u32[]{:S(2)}) collective-permute-start(bf16[672,512]{1,0:T(8,128)(2,1)} %collective-permute-done.9.refs_6_), channel_id=1, source_target_pairs={{0,16},{16,0},{1,17},{17,1},{2,18},{18,2},{3,19},{19,3},{4,20},{20... | collective-permute-start | bytes 2064392 | tf_op jit(solution)/shard_map/ppermute | solution.py:597
  141.9 10.6 %copy-start.4 = (bf16[1344,1024]{1,0:T(8,128)(2,1)S(1)}, bf16[1344,1024]{1,0:T(8,128)(2,1)}, u32[]{:S(2)}) copy-start(bf16[1344,1024]{1,0:T(8,128)(2,1)} %param.14) | copy-start | bytes 8257540
  143.6 8.9 %collective-permute-start.23 = (bf16[1344,128]{1,0:T(8,128)(2,1)S(1)}, bf16[1344,128]{1,0:T(8,128)(2,1)S(1)}, u32[]{:S(2)}, u32[]{:S(2)}) collective-permute-start(bf16[1344,128]{1,0:T(8,128)(2,1)S(1)} %slice.35), channel_id=1, source_target_pairs={{0,8},{4,12},{8,0},{12,4},{1,9},{5,13},{9,1},{13,5},{2,10},{6,14},... | collective-permute-start | bytes 1032200 | tf_op jit(solution)/shard_map/ppermute | solution.py:656
  152.5 85.9 %collective-permute-start.13 = (bf16[1344,1024]{1,0:T(8,128)(2,1)S(1)}, bf16[1344,1024]{1,0:T(8,128)(2,1)}, u32[]{:S(2)}, u32[]{:S(2)}) collective-permute-start(bf16[1344,1024]{1,0:T(8,128)(2,1)S(1)} %bitcast.75), channel_id=1, source_target_pairs={{0,4},{4,0},{8,12},{12,8},{1,5},{5,1},{9,13},{13,9},{2,6},{6,2},{1... | collective-permute-start | bytes 8257544 | tf_op jit(solution)/shard_map/ppermute | solution.py:605
  154.5 35.6 %collective-permute-start.1 = (bf16[1344,512]{1,0:T(8,128)(2,1)}, bf16[1344,512]{1,0:T(8,128)(2,1)}, u32[]{:S(2)}, u32[]{:S(2)}) collective-permute-start(bf16[1344,512]{1,0:T(8,128)(2,1)} %get-tuple-element.26), channel_id=1, source_target_pairs={{0,4},{4,0},{8,12},{12,8},{1,5},{5,1},{9,13},{13,9},{2,6},{6,2},{1... | collective-permute-start | bytes 4128776 | tf_op jit(solution)/shard_map/ppermute | solution.py:595
  155.0 18.5 %collective-permute-start.3 = (bf16[672,512]{1,0:T(8,128)(2,1)}, bf16[672,512]{1,0:T(8,128)(2,1)S(1)}, u32[]{:S(2)}, u32[]{:S(2)}) collective-permute-start(bf16[672,512]{1,0:T(8,128)(2,1)} %collective-permute-done.2.refs_4_), channel_id=1, source_target_pairs={{0,16},{16,0},{1,17},{17,1},{2,18},{18,2},{3,19},{19,3},{4,20},{20... | collective-permute-start | bytes 2064392 | tf_op jit(solution)/shard_map/ppermute | solution.py:596
  156.6 181.8 %reduce-scatter.2.cloned.1.call-start = ((), (), s32[]{:S(2)}) async-start(), calls=%async_computation.1 | async-start | bytes 3440640 | tf_op jit(solution)/shard_map/reduce_scatter | solution.py:701
  156.8 31.6 %collective-permute-start.5 = (bf16[672,512]{1,0:T(8,128)(2,1)}, bf16[672,512]{1,0:T(8,128)(2,1)}, u32[]{:S(2)}, u32[]{:S(2)}) collective-permute-start(bf16[672,512]{1,0:T(8,128)(2,1)} %collective-permute-done.4.refs_6_), channel_id=1, source_target_pairs={{0,16},{16,0},{1,17},{17,1},{2,18},{18,2},{3,19},{19,3},{4,20},{20... | collective-permute-start | bytes 2064392 | tf_op jit(solution)/shard_map/ppermute | solution.py:597
  173.5 12.0 %copy-start.10 = (bf16[672,512]{1,0:T(8,128)(2,1)}, bf16[672,512]{1,0:T(8,128)(2,1)S(1)}, u32[]{:S(2)}) copy-start(bf16[672,512]{1,0:T(8,128)(2,1)S(1)} %collective-permute-done.3.refs_5_) | copy-start | bytes 2064388
  173.5 29.6 %collective-permute-start.15 = (bf16[336,1024]{1,0:T(8,128)(2,1)}, bf16[336,1024]{1,0:T(8,128)(2,1)}, u32[]{:S(2)}, u32[]{:S(2)}) collective-permute-start(bf16[336,1024]{1,0:T(8,128)(2,1)} %collective-permute-done.14.refs_2_), channel_id=1, source_target_pairs={{0,16},{16,0},{1,17},{17,1},{2,18},{18,2},{3,19},{19,3},{4,20},{20... | collective-permute-start | bytes 2064392 | tf_op jit(solution)/shard_map/ppermute | solution.py:610
  174.2 42.7 %collective-permute-start.17 = (bf16[336,1024]{1,0:T(8,128)(2,1)}, bf16[336,1024]{1,0:T(8,128)(2,1)}, u32[]{:S(2)}, u32[]{:S(2)}) collective-permute-start(bf16[336,1024]{1,0:T(8,128)(2,1)} %collective-permute-done.16.refs_4_), channel_id=1, source_target_pairs={{0,16},{16,0},{1,17},{17,1},{2,18},{18,2},{3,19},{19,3},{4,20},{20... | collective-permute-start | bytes 2064392 | tf_op jit(solution)/shard_map/ppermute | solution.py:610
  188.4 28.6 %collective-permute-start.11 = (bf16[512,512]{1,0:T(8,128)(2,1)}, bf16[512,512]{1,0:T(8,128)(2,1)S(1)}, u32[]{:S(2)}, u32[]{:S(2)}) collective-permute-start(bf16[512,512]{1,0:T(8,128)(2,1)} %project.5.k0.v0), channel_id=1, source_target_pairs={{0,8},{4,12},{8,0},{12,4},{1,9},{5,13},{9,1},{13,5},{2,10},{6,14},... | collective-permute-start | bytes 1572872 | tf_op jit(solution)/shard_map/ppermute | solution.py:687
  190.1 48.1 %collective-permute-start.18 = (bf16[336,1024]{1,0:T(8,128)(2,1)}, bf16[336,1024]{1,0:T(8,128)(2,1)}, u32[]{:S(2)}, u32[]{:S(2)}) collective-permute-start(bf16[336,1024]{1,0:T(8,128)(2,1)} %collective-permute-done.14.refs_2_), channel_id=1, source_target_pairs={{0,4},{4,0},{8,12},{12,8},{1,5},{5,1},{9,13},{13,9},{2,6},{6,2},{1... | collective-permute-start | bytes 2064392 | tf_op jit(solution)/shard_map/ppermute | solution.py:612
  203.1 35.3 %collective-permute-start.20 = (bf16[336,1024]{1,0:T(8,128)(2,1)}, bf16[336,1024]{1,0:T(8,128)(2,1)}, u32[]{:S(2)}, u32[]{:S(2)}) collective-permute-start(bf16[336,1024]{1,0:T(8,128)(2,1)} %collective-permute-done.16.refs_4_), channel_id=1, source_target_pairs={{0,4},{4,0},{8,12},{12,8},{1,5},{5,1},{9,13},{13,9},{2,6},{6,2},{1... | collective-permute-start | bytes 2064392 | tf_op jit(solution)/shard_map/ppermute | solution.py:612
  217.0 21.4 %collective-permute-start.19 = (bf16[336,1024]{1,0:T(8,128)(2,1)}, bf16[336,1024]{1,0:T(8,128)(2,1)}, u32[]{:S(2)}, u32[]{:S(2)}) collective-permute-start(bf16[336,1024]{1,0:T(8,128)(2,1)} %collective-permute-done.15.refs_3_), channel_id=1, source_target_pairs={{0,4},{4,0},{8,12},{12,8},{1,5},{5,1},{9,13},{13,9},{2,6},{6,2},{1... | collective-permute-start | bytes 2064392 | tf_op jit(solution)/shard_map/ppermute | solution.py:612
  217.0 9.2 %copy-start.3 = (bf16[512,512]{1,0:T(8,128)(2,1)}, bf16[512,512]{1,0:T(8,128)(2,1)S(1)}, u32[]{:S(2)}) copy-start(bf16[512,512]{1,0:T(8,128)(2,1)S(1)} %collective-permute-done.11.k2.v2) | copy-start | bytes 1572868
  217.0 21.4 %collective-permute-start.21 = (bf16[336,1024]{1,0:T(8,128)(2,1)}, bf16[336,1024]{1,0:T(8,128)(2,1)}, u32[]{:S(2)}, u32[]{:S(2)}) collective-permute-start(bf16[336,1024]{1,0:T(8,128)(2,1)} %collective-permute-done.17.refs_5_), channel_id=1, source_target_pairs={{0,4},{4,0},{8,12},{12,8},{1,5},{5,1},{9,13},{13,9},{2,6},{6,2},{1... | collective-permute-start | bytes 2064392 | tf_op jit(solution)/shard_map/ppermute | solution.py:612
  238.2 1.5 collective-permute-start.12
  239.7 0.7 copy-start.13
  254.5 3.4 collective-permute-start.24
  257.9 1.1 copy-start.5
  279.6 1.3 collective-permute-start.25
  281.0 0.7 copy-start.14
  291.2 15.6 %copy-start.2 = (bf16[4,1344,128]{2,1,0:T(8,128)(2,1)S(1)}, bf16[4,1344,128]{2,1,0:T(8,128)(2,1)}, u32[]{:S(2)}) copy-start(bf16[4,1344,128]{2,1,0:T(8,128)(2,1)} %project_out.3) | copy-start | bytes 4128772
  292.5 14.3 %collective-permute-start.26 = (bf16[1344,128]{1,0:T(8,128)(2,1)S(1)}, bf16[1344,128]{1,0:T(8,128)(2,1)S(1)}, u32[]{:S(2)}, u32[]{:S(2)}) collective-permute-start(bf16[1344,128]{1,0:T(8,128)(2,1)S(1)} %get-tuple-element.33), channel_id=1, source_target_pairs={{0,1},{4,5},{8,9},{12,13},{16,17},{20,21},{24,25},{28,29}} | collective-permute-start | bytes 1032200 | tf_op jit(solution)/shard_map/ppermute | solution.py:566
  294.1 12.7 %collective-permute-start.27 = (bf16[1344,128]{1,0:T(8,128)(2,1)S(1)}, bf16[1344,128]{1,0:T(8,128)(2,1)S(1)}, u32[]{:S(2)}, u32[]{:S(2)}) collective-permute-start(bf16[1344,128]{1,0:T(8,128)(2,1)S(1)} %get-tuple-element.32), channel_id=1, source_target_pairs={{3,2},{7,6},{11,10},{15,14},{19,18},{23,22},{27,26},{31,30}} | collective-permute-start | bytes 1032200 | tf_op jit(solution)/shard_map/ppermute | solution.py:567
  307.0 11.8 %collective-permute-start.28 = (bf16[1344,128]{1,0:T(8,128)(2,1)S(1)}, bf16[1344,128]{1,0:T(8,128)(2,1)S(1)}, u32[]{:S(2)}, u32[]{:S(2)}) collective-permute-start(bf16[1344,128]{1,0:T(8,128)(2,1)S(1)} %get-tuple-element.31), channel_id=1, source_target_pairs={{0,1},{1,2},{4,5},{5,6},{8,9},{9,10},{12,13},{13,14},{16,17},{17,1... | collective-permute-start | bytes 1032200 | tf_op jit(solution)/shard_map/ppermute | solution.py:566
  311.4 7.4 %collective-permute-start.29 = (bf16[1344,128]{1,0:T(8,128)(2,1)S(1)}, bf16[1344,128]{1,0:T(8,128)(2,1)S(1)}, u32[]{:S(2)}, u32[]{:S(2)}) collective-permute-start(bf16[1344,128]{1,0:T(8,128)(2,1)S(1)} %get-tuple-element.30), channel_id=1, source_target_pairs={{3,2},{2,1},{7,6},{6,5},{11,10},{10,9},{15,14},{14,13},{19,18},{18... | collective-permute-start | bytes 1032200 | tf_op jit(solution)/shard_map/ppermute | solution.py:567
  319.0 27.3 %copy-start.6 = (bf16[1344,128]{1,0:T(8,128)(2,1)S(1)}, bf16[1344,128]{1,0:T(8,128)(2,1)}, u32[]{:S(2)}) copy-start(bf16[1344,128]{1,0:T(8,128)(2,1)} %multiply_convert_fusion) | copy-start | bytes 1032196
  319.0 15.0 %collective-permute-start.30 = (bf16[1344,128]{1,0:T(8,128)(2,1)S(1)}, bf16[1344,128]{1,0:T(8,128)(2,1)S(1)}, u32[]{:S(2)}, u32[]{:S(2)}) collective-permute-start(bf16[1344,128]{1,0:T(8,128)(2,1)S(1)} %get-tuple-element.29), channel_id=1, source_target_pairs={{0,1},{1,2},{2,3},{4,5},{5,6},{6,7},{8,9},{9,10},{10,11},{12,13},{... | collective-permute-start | bytes 1032200 | tf_op jit(solution)/shard_map/ppermute | solution.py:566
  327.8 10.3 %collective-permute-start.31 = (bf16[1344,128]{1,0:T(8,128)(2,1)S(1)}, bf16[1344,128]{1,0:T(8,128)(2,1)S(1)}, u32[]{:S(2)}, u32[]{:S(2)}) collective-permute-start(bf16[1344,128]{1,0:T(8,128)(2,1)S(1)} %get-tuple-element.28), channel_id=1, source_target_pairs={{3,2},{2,1},{1,0},{7,6},{6,5},{5,4},{11,10},{10,9},{9,8},{15,14},{... | collective-permute-start | bytes 1032200 | tf_op jit(solution)/shard_map/ppermute | solution.py:567
  338.2 0.7 copy-start.11
  340.2 9.9 %copy-start.7 = (bf16[256,1344]{0,1:T(8,128)(2,1)S(1)}, bf16[256,1344]{0,1:T(8,128)(2,1)}, u32[]{:S(2)}) copy-start(bf16[256,1344]{0,1:T(8,128)(2,1)} %param.10) | copy-start | bytes 2064388
  340.2 9.9 %copy-start.8 = (bf16[1,1344,256]{2,1,0:T(8,128)(2,1)S(1)}, bf16[1,1344,256]{2,1,0:T(8,128)(2,1)}, u32[]{:S(2)}) copy-start(bf16[1,1344,256]{2,1,0:T(8,128)(2,1)} %reduce-scatter.2.cloned.1.call-done) | copy-start | bytes 2064388
  340.2 5.4 %collective-permute-start.32 = (f32[1,384]{1,0:T(1,128)S(1)}, f32[1,384]{1,0:T(1,128)S(1)}, u32[]{:S(2)}, u32[]{:S(2)}) collective-permute-start(f32[1,384]{1,0:T(1,128)S(1)} %pad_maximum_fusion), channel_id=1, source_target_pairs={{0,1},{1,2},{2,3},{3,0},{4,5},{5,6},{6,7},{7,4},{8,9},{9,10},{10,1... | collective-permute-start | bytes 4616 | tf_op jit(solution)/shard_map/ppermute | solution.py:579
  340.6 5.1 %collective-permute-start.33 = (f32[1,384]{1,0:T(1,128)S(1)}, f32[1,384]{1,0:T(1,128)S(1)}, u32[]{:S(2)}, u32[]{:S(2)}) collective-permute-start(f32[1,384]{1,0:T(1,128)S(1)} %pad_maximum_fusion), channel_id=1, source_target_pairs={{0,2},{1,3},{2,0},{3,1},{4,6},{5,7},{6,4},{7,5},{8,10},{9,11},{10,... | collective-permute-start | bytes 4616 | tf_op jit(solution)/shard_map/ppermute | solution.py:579
  340.6 5.7 %collective-permute-start.34 = (f32[1,384]{1,0:T(1,128)S(1)}, f32[1,384]{1,0:T(1,128)S(1)}, u32[]{:S(2)}, u32[]{:S(2)}) collective-permute-start(f32[1,384]{1,0:T(1,128)S(1)} %pad_maximum_fusion), channel_id=1, source_target_pairs={{0,3},{1,0},{2,1},{3,2},{4,7},{5,4},{6,5},{7,6},{8,11},{9,8},{10,9... | collective-permute-start | bytes 4616 | tf_op jit(solution)/shard_map/ppermute | solution.py:579
Sparse Core Ops, SparseCore 0:
  9.5 59.6 all-gather.4
  156.7 32.4 all-gather.6
  250.7 55.6 reduce-scatter.1

commit v3 on v2

--- a/solution.py
+++ b/solution.py
@@ -549,26 +549,18 @@
     )(pos, mine, theirs, own, core, *near, *far)
 
 
-def line_scatter(parts, axis):
+def direct_scatter(parts, axis):
     count = lax.axis_size(axis)
     index = lax.axis_index(axis)
 
     def block(at):
-        return lax.dynamic_index_in_dim(parts, jnp.clip(at, 0, count - 1), 0, False)
-
-    a = b = None
-    for step in range(1, count):
-        far = count - step
-        send_a, send_b = block(index + far), block(index - far)
-        if a is not None:
-            send_a = (send_a.astype(jnp.float32) + a.astype(jnp.float32)).astype(jnp.bfloat16)
-            send_b = (send_b.astype(jnp.float32) + b.astype(jnp.float32)).astype(jnp.bfloat16)
-        a = lax.ppermute(send_a, axis, [(i, i + 1) for i in range(step)])
-        b = lax.ppermute(send_b, axis, [(count - 1 - i, count - 2 - i) for i in range(step)])
-        a, b = lax.optimization_barrier((a, b))
-    return (
-        block(index).astype(jnp.float32) + a.astype(jnp.float32) + b.astype(jnp.float32)
-    )
+        return lax.dynamic_index_in_dim(parts, at % count, 0, False)
+
+    got = [
+        lax.ppermute(block(index + by), axis, [(i, (i + by) % count) for i in range(count)])
+        for by in range(1, count)
+    ]
+    return sum((part.astype(jnp.float32) for part in got), block(index).astype(jnp.float32))
 
 
 def total_over(value, axis):
@@ -699,10 +691,10 @@
     gain_part = lax.dynamic_slice_in_dim(post_gain, tp_index * local_cols, local_cols)[:, None]
 
     attn_p = lax.psum_scatter(part_p, "tp", scatter_dimension=0).astype(jnp.float32)
-    attn_c = line_scatter(part_c, "tp")
-    row_sq = jnp.concatenate(
-        [jnp.sum(attn * attn, axis=0, keepdims=True) for attn in (attn_p, attn_c)], axis=1
-    )
+    attn_c = direct_scatter(part_c, "tp")
+    sum_p = jnp.sum(attn_p * attn_p, axis=0, keepdims=True)
+    sum_c = jnp.sum(attn_c * attn_c, axis=0, keepdims=True)
+    row_sq = jnp.concatenate([sum_p, sum_c], axis=1)
     factor = lax.rsqrt(total_over(row_sq, "tp") / full_width + eps_norm)
 
     def finish(attn, factor, rows_t):

time: 359 us -> 352 us (0.981)
  starting transfers between devices: 46.8 us -> 39.8 us
    ppermute x6 -> x3, starting transfers between devices: 17.5 us -> 4.01 us  [direct_scatter(): lax.ppermute(block(index + by), axis, [(i, (i + by) % count) for i in ran...]
    ppermute x3, starting transfers between devices: 3.88 us -> 10.4 us  [total_over(): total = total + lax.ppermute(value, axis, pairs)]
    ppermute x6 -> x3, waiting for transfers between devices: 27.7 us -> 27 us  [direct_scatter(): lax.ppermute(block(index + by), axis, [(i, (i + by) % count) for i in ran...]
  transfers between devices with their start and end apart: 38 -> 35, of which waited for: 18 -> 16; matrix products, arithmetic and copies ran while one was open for 10% -> 10% of each run, Pallas kernels for 28% -> 28%
where the time goes in v3:
time: 352 us; the launch traced here: 350 us
  waiting for transfers between devices  151 us (43%)
  Pallas kernels  99.7 us (28%)
  starting transfers between devices  39.8 us (11%)
  local copies, waits for them, and re-layouts  28.7 us (8%)
  other arithmetic  17.5 us (5%)
  between operations  14.1 us (4%)
    pallas_call x4, Pallas kernels, project(): pl.pallas_call(functools.partial(proj_kernel, normed_cols, len(sources),...  28.9 us
    ppermute x3, waiting for transfers between devices, direct_scatter(): lax.ppermute(block(index + by), axis, [(i, (i + by) % count) for i in ran...  27 us
    ppermute x2, waiting for transfers between devices, full_pieces(): more = lax.ppermute(got, 'grp', ACROSS)  26.8 us
    pallas_call x2, Pallas kernels, pick_rows(): pl.pallas_call(pick_kernel, out_shape=jax.ShapeDtypeStruct((width, rows),...  25.3 us
    all_gather x1, waiting for transfers between devices, paired_device(): prompt_x = lax.all_gather(prompt_t, 'tp', axis=0)  23 us
    pallas_call x2, Pallas kernels, project_out(): pl.pallas_call(functools.partial(out_kernel, len(near)), out_shape=jax.Sh...  19.5 us
    pallas_call x2, Pallas kernels, attend_rows(): pl.pallas_call(kernel, out_shape=jax.ShapeDtypeStruct((2, rows, q_cols),...  17.1 us
    ppermute x2, waiting for transfers between devices, half_pieces(): near_x = lax.ppermute(near, 'grp', ACROSS)  15.3 us
  transfers between devices with their start and end apart: 35, of which 16 were waited for; matrix products, arithmetic and copies ran while one was open for 10% of the time, Pallas kernels for 28%

profile of v3, /device:TPU:0, one launch (start us, length us, event | category | flops | bytes accessed | tf_op | source)
XLA Modules:
  0.0 350.5 jit_solution(11187740024126000021)
XLA Ops:
  9.8 0.8 copy.17.listed
  13.3 1.9 pad_add_fusion
  15.3 12.0 %pick_rows.3 = bf16[1344,256]{1,0:T(8,128)(2,1)} custom-call(s32[265]{0:T(512)} %get-tuple-element.35.info, bf16[1344,32768]{1,0:T(8,128)(2,1)} %bitcast.18.emb, s32[2,128]{1,0:T(2,128)} %get-tuple-element.31.lanes, s32[256,1]{1,0:T(8,128)} %copy.17.listed, s32[1,256]{1,0:T(1,128)} %and_select_fusion.ids), custom_call_target="tpu_custom_call" | custom-call | tf_op jit(solution)/shard_map/pick_rows/pallas_call | solution.py:272
  27.3 2.3 collective-permute-start.22
  29.6 3.6 %constant_dynamic-slice_fusion.6 = (bf16[1344,2,256]{2,1,0:T(2,128)(2,1)S(1)}, bf16[1344,2,256]{2,1,0:T(2,128)(2,1)S(1)}) fusion(bf16[1344,2,512]{2,1,0:T(2,128)(2,1)} %param.15, s32[]{:T(128)S(6)} %select_n.229, s32[]{:T(128)S(6)} %select_n.228), kind=kLoop, calls=%fused_computation.51 | loop fusion | bytes 5505032 | tf_op jit(solution)/shard_map/dynamic_slice | solution.py:633
  33.6 1.0 constant_dynamic-slice_fusion.5
  34.6 6.8 %collective-permute-start.7 = (bf16[672,512]{1,0:T(8,128)(2,1)}, bf16[672,512]{1,0:T(8,128)(2,1)S(1)}, u32[]{:S(2)}, u32[]{:S(2)}) collective-permute-start(bf16[672,512]{1,0:T(8,128)(2,1)} %constant_dynamic-slice_fusion.5), channel_id=1, source_target_pairs={{0,8},{4,12},{8,0},{12,4},{1,9},{5,13},{9,1},{13,5},{2,10},{6,14},... | collective-permute-start | bytes 2064392 | tf_op jit(solution)/shard_map/ppermute | solution.py:585
  41.3 1.4 copy.20
  42.8 2.0 constant_dynamic-slice_fusion.4
  46.2 23.0 %all-gather.5.cloned.1.call-done = bf16[5376,256]{1,0:T(8,128)(2,1)} async-done(((bf16[1344,256]{1,0:T(8,128)(2,1)}), bf16[5376,256]{1,0:T(8,128)(2,1)}) %all-gather.5.cloned.1.call-update) | async-done | bytes 2752528 | tf_op jit(solution)/shard_map/all_gather | solution.py:629
  69.2 5.1 %norm_rows.2.refs_0_ = bf16[256,5632]{1,0:T(8,128)(2,1)} custom-call(s32[3]{0:T(128)} %pad_add_fusion.2.pos, f32[4,1344]{1,0:T(4,128)} %reshape.279.gain, bf16[4,1344,256]{2,1,0:T(8,128)(2,1)} %bitcast.74), custom_call_target="tpu_custom_call" | custom-call | tf_op jit(solution)/shard_map/norm_rows/pallas_call | solution.py:315
  74.3 3.4 fusion.32
  77.7 1.5 collective-permute-start.2
  79.2 1.0 dynamic-slice_bitcast_fusion
  80.9 1.5 collective-permute-start.14
  82.9 13.4 %collective-permute-done.2.refs_4_ = bf16[672,512]{1,0:T(8,128)(2,1)} collective-permute-done((bf16[672,512]{1,0:T(8,128)(2,1)}, bf16[672,512]{1,0:T(8,128)(2,1)}, u32[]{:S(2)}, u32[]{:S(2)}) %collective-permute-start.2) | collective-permute-done | bytes 688160 | tf_op jit(solution)/shard_map/ppermute | solution.py:585
  96.3 13.8 %collective-permute-done.4.refs_6_ = bf16[672,512]{1,0:T(8,128)(2,1)} collective-permute-done((bf16[672,512]{1,0:T(8,128)(2,1)S(1)}, bf16[672,512]{1,0:T(8,128)(2,1)}, u32[]{:S(2)}, u32[]{:S(2)}) %collective-permute-start.4) | collective-permute-done | bytes 688160 | tf_op jit(solution)/shard_map/ppermute | solution.py:586
  110.1 1.5 collective-permute-start.8
  111.6 14.2 %collective-permute-done.14.refs_2_ = bf16[336,1024]{1,0:T(8,128)(2,1)} collective-permute-done((bf16[336,1024]{1,0:T(8,128)(2,1)S(1)}, bf16[336,1024]{1,0:T(8,128)(2,1)}, u32[]{:S(2)}, u32[]{:S(2)}) %collective-permute-start.14) | collective-permute-done | bytes 688160 | tf_op jit(solution)/shard_map/ppermute | solution.py:601
  125.8 1.5 collective-permute-start.10
  127.9 0.8 copy.16.listed
  128.7 13.2 %pick_rows.2 = bf16[1344,256]{1,0:T(8,128)(2,1)} custom-call(s32[265]{0:T(512)} %get-tuple-element.36.info, bf16[1344,32768]{1,0:T(8,128)(2,1)} %bitcast.18.emb, s32[2,128]{1,0:T(2,128)} %get-tuple-element.33.lanes, s32[256,1]{1,0:T(8,128)} %copy.16.listed, s32[1,256]{1,0:T(1,128)} %and_select_fusion.1.ids), custom_call_target="tpu_custom_call" | custom-call | tf_op jit(solution)/shard_map/pick_rows/pallas_call | solution.py:272
  141.9 1.6 add.206
  143.6 1.7 collective-permute-start.23
  145.3 7.2 %collective-permute-done.23 = bf16[1344,128]{1,0:T(8,128)(2,1)S(1)} collective-permute-done((bf16[1344,128]{1,0:T(8,128)(2,1)S(1)}, bf16[1344,128]{1,0:T(8,128)(2,1)S(1)}, u32[]{:S(2)}, u32[]{:S(2)}) %collective-permute-start.23) | collective-permute-done | bytes 344096 | tf_op jit(solution)/shard_map/ppermute | solution.py:648
  152.5 1.8 constant_dynamic-slice_fusion.8
  155.6 0.8 multiply_convert_fusion
  156.7 1.4 collective-permute-start.5
  158.1 15.3 %collective-permute-done.3.refs_5_ = bf16[672,512]{1,0:T(8,128)(2,1)S(1)} collective-permute-done((bf16[672,512]{1,0:T(8,128)(2,1)}, bf16[672,512]{1,0:T(8,128)(2,1)S(1)}, u32[]{:S(2)}, u32[]{:S(2)}) %collective-permute-start.3) | collective-permute-done | bytes 688160 | tf_op jit(solution)/shard_map/ppermute | solution.py:588
  174.1 1.3 collective-permute-start.17
  175.4 1.8 fusion.8
  177.2 8.1 %project.5.k0.v0 = bf16[512,512]{1,0:T(8,128)(2,1)} custom-call(s32[3]{0:T(128)} %pad_add_fusion.2.pos, f32[1,128]{1,0:T(1,128)} %bitcast.89, f32[512,128]{1,0:T(8,128)} %get-tuple-element.24.cosine, f32[512,128]{1,0:T(8,128)} %get-tuple-element.23.sine, bf16[256,5632]{1,0:T(8,128)(2,1)} %norm_rows.2.refs_0_, ...), custom_call_target="tpu_custom_call" | custom-call | tf_op jit(solution)/shard_map/project/pallas_call | solution.py:390
  185.4 2.9 collective-permute-done.5.refs_7_
  188.2 1.7 collective-permute-start.11
  190.0 13.0 %collective-permute-done.15.refs_3_ = bf16[336,1024]{1,0:T(8,128)(2,1)} collective-permute-done((bf16[336,1024]{1,0:T(8,128)(2,1)}, bf16[336,1024]{1,0:T(8,128)(2,1)}, u32[]{:S(2)}, u32[]{:S(2)}) %collective-permute-start.15) | collective-permute-done | bytes 688160 | tf_op jit(solution)/shard_map/ppermute | solution.py:602
  203.0 13.8 %collective-permute-done.17.refs_5_ = bf16[336,1024]{1,0:T(8,128)(2,1)} collective-permute-done((bf16[336,1024]{1,0:T(8,128)(2,1)}, bf16[336,1024]{1,0:T(8,128)(2,1)}, u32[]{:S(2)}, u32[]{:S(2)}) %collective-permute-start.17) | collective-permute-done | bytes 688160 | tf_op jit(solution)/shard_map/ppermute | solution.py:602
  217.3 8.6 %project.4.q = bf16[512,512]{1,0:T(8,128)(2,1)} custom-call(s32[3]{0:T(128)} %pad_add_fusion.2.pos, f32[1,128]{1,0:T(1,128)} %bitcast.91, f32[512,128]{1,0:T(8,128)} %get-tuple-element.24.cosine, f32[512,128]{1,0:T(8,128)} %get-tuple-element.23.sine, bf16[256,5632]{1,0:T(8,128)(2,1)} %norm_rows.2.refs_0_, bf16[256,5632]{1,0:T(8,128)(2,1)} %collective-permute-done.refs_1_, ...), custom_call_target="tpu_custom_call" | custom-call | tf_op jit(solution)/shard_map/project/pallas_call | solution.py:390
  226.0 10.2 %attend_rows.2 = bf16[2,256,512]{2,1,0:T(8,128)(2,1)} custom-call(s32[3]{0:T(128)} %pad_add_fusion.2.pos, bf16[512,512]{1,0:T(8,128)(2,1)} %project.4.q, bf16[512,512]{1,0:T(8,128)(2,1)} %project.5.k0.v0, bf16[512,512]{1,0:T(8,128)(2,1)} %copy-done.2, bf16[512,512]{1,0:T(8,128)(2,1)} %project.5.k0.v0, bf16[512,512]{1,0:T(8,128)(2,1)} %copy-done.2), custom_call_target="tpu_custom_call" | custom-call | tf_op jit(solution)/shard_map/attend_rows/pallas_call | solution.py:490
  236.3 1.8 slice_bitcast_fusion
  238.3 1.3 collective-permute-done.12.theirs
  240.3 10.0 %project_out.2 = bf16[4,1344,256]{2,1,0:T(8,128)(2,1)} custom-call(s32[3]{0:T(128)} %pad_add_fusion.2.pos, bf16[256,512]{1,0:T(8,128)(2,1)} %get-tuple-element.20.mine, bf16[256,512]{1,0:T(8,128)(2,1)} %copy-done.14, bf16[1344,1024]{1,0:T(8,128)(2,1)} %bitcast.66, bf16[1344,1024]{1,0:T(8,128)(2,1)} %collective-permute-done.13.refs_1_, ...), custom_call_target="tpu_custom_call" | custom-call | tf_op jit(solution)/shard_map/project_out/pallas_call | solution.py:536
  250.4 3.8 %norm_rows.3.refs_0_ = bf16[128,5632]{1,0:T(8,128)(2,1)} custom-call(s32[3]{0:T(128)} %pad_add_fusion.2.pos, f32[4,1344]{1,0:T(4,128)} %reshape.279.gain, bf16[4,1344,128]{2,1,0:T(8,128)(2,1)} %bitcast.76), custom_call_target="tpu_custom_call" | custom-call | tf_op jit(solution)/shard_map/norm_rows/pallas_call | solution.py:315
  254.4 1.3 fusion.17
  255.7 1.9 collective-permute-done.24.refs_1_
  257.6 1.1 copy-done.5
  258.7 6.0 %project.7.ck.cv = bf16[256,512]{1,0:T(8,128)(2,1)} custom-call(s32[3]{0:T(128)} %pad_add_fusion.2.pos, f32[1,128]{1,0:T(1,128)} %bitcast.90, f32[256,128]{1,0:T(8,128)} %get-tuple-element.30.cosine, f32[256,128]{1,0:T(8,128)} %get-tuple-element.29.sine, bf16[128,5632]{1,0:T(8,128)(2,1)} %norm_rows.3.refs_0_, bf16[128,5632]{1,0:T(8,128)(2,1)} %copy-done.5, ...), custom_call_target="tpu_custom_call" | custom-call | tf_op jit(solution)/shard_map/project/pallas_call | solution.py:390
  264.7 6.1 %project.6.q = bf16[256,512]{1,0:T(8,128)(2,1)} custom-call(s32[3]{0:T(128)} %pad_add_fusion.2.pos, f32[1,128]{1,0:T(1,128)} %bitcast.92, f32[256,128]{1,0:T(8,128)} %get-tuple-element.30.cosine, f32[256,128]{1,0:T(8,128)} %get-tuple-element.29.sine, bf16[128,5632]{1,0:T(8,128)(2,1)} %norm_rows.3.refs_0_, bf16[128,5632]{1,0:T(8,128)(2,1)} %copy-done.5, ...), custom_call_target="tpu_custom_call" | custom-call | tf_op jit(solution)/shard_map/project/pallas_call | solution.py:390
  270.8 6.9 %attend_rows.3 = bf16[2,128,512]{2,1,0:T(8,128)(2,1)} custom-call(s32[3]{0:T(128)} %pad_add_fusion.2.pos, bf16[256,512]{1,0:T(8,128)(2,1)} %project.6.q, bf16[512,512]{1,0:T(8,128)(2,1)} %project.5.k0.v0, bf16[512,512]{1,0:T(8,128)(2,1)} %copy-done.2, bf16[512,512]{1,0:T(8,128)(2,1)} %project.5.k0.v0, bf16[512,512]{1,0:T(8,128)(2,1)} %copy-done.2, ...), custom_call_target="tpu_custom_call" | custom-call | tf_op jit(solution)/shard_map/attend_rows/pallas_call | solution.py:490
  277.7 1.6 slice_bitcast_fusion.2
  279.5 1.2 collective-permute-done.25.theirs
  281.4 9.5 %project_out.3 = bf16[4,1344,128]{2,1,0:T(8,128)(2,1)} custom-call(s32[3]{0:T(128)} %pad_add_fusion.2.pos, bf16[128,512]{1,0:T(8,128)(2,1)} %get-tuple-element.22.mine, bf16[128,512]{1,0:T(8,128)(2,1)} %copy-done.15, bf16[1344,1024]{1,0:T(8,128)(2,1)} %bitcast.67, bf16[1344,1024]{1,0:T(8,128)(2,1)} %collective-permute-done.13.refs_1_, ...), custom_call_target="tpu_custom_call" | custom-call | tf_op jit(solution)/shard_map/project_out/pallas_call | solution.py:536
  290.9 2.1 dynamic-slice_bitcast_fusion.4
  293.0 1.5 collective-permute-start.27
  294.5 2.5 collective-permute-start.28
  297.0 13.8 %collective-permute-done.26 = bf16[1344,128]{1,0:T(8,128)(2,1)S(1)} collective-permute-done((bf16[1344,128]{1,0:T(8,128)(2,1)}, bf16[1344,128]{1,0:T(8,128)(2,1)S(1)}, u32[]{:S(2)}, u32[]{:S(2)}) %collective-permute-start.26) | collective-permute-done | bytes 344096 | tf_op jit(solution)/shard_map/ppermute | solution.py:560
  310.8 13.1 %collective-permute-done.27 = bf16[1344,128]{1,0:T(8,128)(2,1)S(1)} collective-permute-done((bf16[1344,128]{1,0:T(8,128)(2,1)S(1)}, bf16[1344,128]{1,0:T(8,128)(2,1)S(1)}, u32[]{:S(2)}, u32[]{:S(2)}) %collective-permute-start.27) | collective-permute-done | bytes 344096 | tf_op jit(solution)/shard_map/ppermute | solution.py:560
  324.2 1.3 fusion
  325.5 8.0 %collective-permute-start.29 = (f32[1,384]{1,0:T(1,128)S(1)}, f32[1,384]{1,0:T(1,128)S(1)}, u32[]{:S(2)}, u32[]{:S(2)}) collective-permute-start(f32[1,384]{1,0:T(1,128)S(1)} %pad_maximum_fusion), channel_id=1, source_target_pairs={{0,1},{1,2},{2,3},{3,0},{4,5},{5,6},{6,7},{7,4},{8,9},{9,10},{10,1... | collective-permute-start | bytes 4616 | tf_op jit(solution)/shard_map/ppermute | solution.py:571
  333.5 1.5 collective-permute-start.30
  335.0 1.0 collective-permute-start.31
  336.7 1.3 collective-permute-done.30
  338.6 2.2 fusion.7
  340.8 1.9 copy.18
  342.7 1.2 fusion.4
  (105 shorter events, 15.3 us)
Async XLA Ops:
  7.2 62.1 %all-gather.5.cloned.1.call-start = ((), (), s32[]{:S(2)}) async-start(), calls=%async_computation.2 | async-start | bytes 3440640 | tf_op jit(solution)/shard_map/all_gather | solution.py:629
  7.9 242.5 %all-gather.7.cloned.1.call-start = ((), (), s32[]{:S(2)}) async-start(), calls=%async_computation.3 | async-start | bytes 1720320 | tf_op jit(solution)/shard_map/all_gather | solution.py:651
  27.3 52.8 %collective-permute-start.22 = (bf16[1344,256]{1,0:T(8,128)(2,1)}, bf16[1344,256]{1,0:T(8,128)(2,1)}, u32[]{:S(2)}, u32[]{:S(2)}) collective-permute-start(bf16[1344,256]{1,0:T(8,128)(2,1)} %pick_rows.3), channel_id=1, source_target_pairs={{0,4},{4,0},{8,12},{12,8},{1,5},{5,1},{9,13},{13,9},{2,6},{6,2},{1... | collective-permute-start | bytes 2064392 | tf_op jit(solution)/shard_map/ppermute | solution.py:647
  33.5 9.2 %copy-start.1 = (bf16[168,8,2,256]{3,1,2,0:T(8,128)(2,1)}, bf16[168,8,2,256]{3,1,2,0:T(8,128)(2,1)S(1)}, u32[]{:S(2)}) copy-start(bf16[168,8,2,256]{3,1,2,0:T(8,128)(2,1)S(1)} %copy.19) | copy-start | bytes 4128772
  34.6 46.3 %collective-permute-start.7 = (bf16[672,512]{1,0:T(8,128)(2,1)}, bf16[672,512]{1,0:T(8,128)(2,1)S(1)}, u32[]{:S(2)}, u32[]{:S(2)}) collective-permute-start(bf16[672,512]{1,0:T(8,128)(2,1)} %constant_dynamic-slice_fusion.5), channel_id=1, source_target_pairs={{0,8},{4,12},{8,0},{12,4},{1,9},{5,13},{9,1},{13,5},{2,10},{6,14},... | collective-permute-start | bytes 2064392 | tf_op jit(solution)/shard_map/ppermute | solution.py:585
  42.8 2.1 copy-start.16
  44.8 37.6 %collective-permute-start.9 = (bf16[672,512]{1,0:T(8,128)(2,1)}, bf16[672,512]{1,0:T(8,128)(2,1)}, u32[]{:S(2)}, u32[]{:S(2)}) collective-permute-start(bf16[672,512]{1,0:T(8,128)(2,1)} %constant_dynamic-slice_fusion.4), channel_id=1, source_target_pairs={{0,12},{4,8},{8,4},{12,0},{1,13},{5,9},{9,5},{13,1},{2,14},{6,10},... | collective-permute-start | bytes 2064392 | tf_op jit(solution)/shard_map/ppermute | solution.py:586
  74.3 99.8 %collective-permute-start = (bf16[256,5632]{1,0:T(8,128)(2,1)}, bf16[256,5632]{1,0:T(8,128)(2,1)}, u32[]{:S(2)}, u32[]{:S(2)}) collective-permute-start(bf16[256,5632]{1,0:T(8,128)(2,1)} %norm_rows.2.refs_0_), channel_id=1, source_target_pairs={{0,4},{4,0},{8,12},{12,8},{1,5},{5,1},{9,13},{13,9},{2,6},{6,2},{1... | collective-permute-start | bytes 8650760 | tf_op jit(solution)/shard_map/ppermute | solution.py:672
  74.3 4.8 %copy-start = (bf16[1024,1344]{0,1:T(8,128)(2,1)S(1)}, bf16[1024,1344]{0,1:T(8,128)(2,1)}, u32[]{:S(2)}) copy-start(bf16[1024,1344]{0,1:T(8,128)(2,1)} %param.18) | copy-start | bytes 8257540
  77.7 18.6 %collective-permute-start.2 = (bf16[672,512]{1,0:T(8,128)(2,1)}, bf16[672,512]{1,0:T(8,128)(2,1)}, u32[]{:S(2)}, u32[]{:S(2)}) collective-permute-start(bf16[672,512]{1,0:T(8,128)(2,1)} %get-tuple-element.13), channel_id=1, source_target_pairs={{0,8},{4,12},{8,0},{12,4},{1,9},{5,13},{9,1},{13,5},{2,10},{6,14},... | collective-permute-start | bytes 2064392 | tf_op jit(solution)/shard_map/ppermute | solution.py:585
  79.2 1.3 copy-start.13
  80.5 29.6 %collective-permute-start.4 = (bf16[672,512]{1,0:T(8,128)(2,1)S(1)}, bf16[672,512]{1,0:T(8,128)(2,1)}, u32[]{:S(2)}, u32[]{:S(2)}) collective-permute-start(bf16[672,512]{1,0:T(8,128)(2,1)S(1)} %copy-done.13), channel_id=1, source_target_pairs={{0,12},{4,8},{8,4},{12,0},{1,13},{5,9},{9,5},{13,1},{2,14},{6,10},... | collective-permute-start | bytes 2064392 | tf_op jit(solution)/shard_map/ppermute | solution.py:586
  80.9 61.0 %copy-start.9 = (bf16[672,512]{1,0:T(8,128)(2,1)}, bf16[672,512]{1,0:T(8,128)(2,1)S(1)}, u32[]{:S(2)}) copy-start(bf16[672,512]{1,0:T(8,128)(2,1)S(1)} %collective-permute-done.7.refs_4_) | copy-start | bytes 2064388
  80.9 44.9 %collective-permute-start.14 = (bf16[336,1024]{1,0:T(8,128)(2,1)S(1)}, bf16[336,1024]{1,0:T(8,128)(2,1)}, u32[]{:S(2)}, u32[]{:S(2)}) collective-permute-start(bf16[336,1024]{1,0:T(8,128)(2,1)S(1)} %get-tuple-element.9), channel_id=1, source_target_pairs={{0,8},{4,12},{8,0},{12,4},{1,9},{5,13},{9,1},{13,5},{2,10},{6,14},... | collective-permute-start | bytes 2064392 | tf_op jit(solution)/shard_map/ppermute | solution.py:601
  82.4 61.2 %collective-permute-start.16 = (bf16[336,1024]{1,0:T(8,128)(2,1)}, bf16[336,1024]{1,0:T(8,128)(2,1)}, u32[]{:S(2)}, u32[]{:S(2)}) collective-permute-start(bf16[336,1024]{1,0:T(8,128)(2,1)} %get-tuple-element.8), channel_id=1, source_target_pairs={{0,8},{4,12},{8,0},{12,4},{1,9},{5,13},{9,1},{13,5},{2,10},{6,14},... | collective-permute-start | bytes 2064392 | tf_op jit(solution)/shard_map/ppermute | solution.py:601
  96.3 60.3 %collective-permute-start.6 = (bf16[1344,512]{1,0:T(8,128)(2,1)}, bf16[1344,512]{1,0:T(8,128)(2,1)}, u32[]{:S(2)}, u32[]{:S(2)}) collective-permute-start(bf16[1344,512]{1,0:T(8,128)(2,1)} %bitcast.43), channel_id=1, source_target_pairs={{0,4},{4,0},{8,12},{12,8},{1,5},{5,1},{9,13},{13,9},{2,6},{6,2},{1... | collective-permute-start | bytes 4128776 | tf_op jit(solution)/shard_map/ppermute | solution.py:587
  110.1 44.2 %collective-permute-start.8 = (bf16[672,512]{1,0:T(8,128)(2,1)S(1)}, bf16[672,512]{1,0:T(8,128)(2,1)}, u32[]{:S(2)}, u32[]{:S(2)}) collective-permute-start(bf16[672,512]{1,0:T(8,128)(2,1)S(1)} %collective-permute-done.7.refs_4_), channel_id=1, source_target_pairs={{0,16},{16,0},{1,17},{17,1},{2,18},{18,2},{3,19},{19,3},{4,20},{20... | collective-permute-start | bytes 2064392 | tf_op jit(solution)/shard_map/ppermute | solution.py:588
  125.8 29.0 %collective-permute-start.10 = (bf16[672,512]{1,0:T(8,128)(2,1)}, bf16[672,512]{1,0:T(8,128)(2,1)}, u32[]{:S(2)}, u32[]{:S(2)}) collective-permute-start(bf16[672,512]{1,0:T(8,128)(2,1)} %collective-permute-done.9.refs_6_), channel_id=1, source_target_pairs={{0,16},{16,0},{1,17},{17,1},{2,18},{18,2},{3,19},{19,3},{4,20},{20... | collective-permute-start | bytes 2064392 | tf_op jit(solution)/shard_map/ppermute | solution.py:589
  141.9 10.6 %copy-start.4 = (bf16[1344,1024]{1,0:T(8,128)(2,1)S(1)}, bf16[1344,1024]{1,0:T(8,128)(2,1)}, u32[]{:S(2)}) copy-start(bf16[1344,1024]{1,0:T(8,128)(2,1)} %param.14) | copy-start | bytes 8257540
  143.6 8.9 %collective-permute-start.23 = (bf16[1344,128]{1,0:T(8,128)(2,1)S(1)}, bf16[1344,128]{1,0:T(8,128)(2,1)S(1)}, u32[]{:S(2)}, u32[]{:S(2)}) collective-permute-start(bf16[1344,128]{1,0:T(8,128)(2,1)S(1)} %slice.35), channel_id=1, source_target_pairs={{0,8},{4,12},{8,0},{12,4},{1,9},{5,13},{9,1},{13,5},{2,10},{6,14},... | collective-permute-start | bytes 1032200 | tf_op jit(solution)/shard_map/ppermute | solution.py:648
  152.5 85.8 %collective-permute-start.13 = (bf16[1344,1024]{1,0:T(8,128)(2,1)S(1)}, bf16[1344,1024]{1,0:T(8,128)(2,1)}, u32[]{:S(2)}, u32[]{:S(2)}) collective-permute-start(bf16[1344,1024]{1,0:T(8,128)(2,1)S(1)} %bitcast.68), channel_id=1, source_target_pairs={{0,4},{4,0},{8,12},{12,8},{1,5},{5,1},{9,13},{13,9},{2,6},{6,2},{1... | collective-permute-start | bytes 8257544 | tf_op jit(solution)/shard_map/ppermute | solution.py:597
  154.4 35.6 %collective-permute-start.1 = (bf16[1344,512]{1,0:T(8,128)(2,1)}, bf16[1344,512]{1,0:T(8,128)(2,1)}, u32[]{:S(2)}, u32[]{:S(2)}) collective-permute-start(bf16[1344,512]{1,0:T(8,128)(2,1)} %get-tuple-element.14), channel_id=1, source_target_pairs={{0,4},{4,0},{8,12},{12,8},{1,5},{5,1},{9,13},{13,9},{2,6},{6,2},{1... | collective-permute-start | bytes 4128776 | tf_op jit(solution)/shard_map/ppermute | solution.py:587
  154.9 18.5 %collective-permute-start.3 = (bf16[672,512]{1,0:T(8,128)(2,1)}, bf16[672,512]{1,0:T(8,128)(2,1)S(1)}, u32[]{:S(2)}, u32[]{:S(2)}) collective-permute-start(bf16[672,512]{1,0:T(8,128)(2,1)} %collective-permute-done.2.refs_4_), channel_id=1, source_target_pairs={{0,16},{16,0},{1,17},{17,1},{2,18},{18,2},{3,19},{19,3},{4,20},{20... | collective-permute-start | bytes 2064392 | tf_op jit(solution)/shard_map/ppermute | solution.py:588
  156.4 167.8 %reduce-scatter.2.cloned.1.call-start = ((), (), s32[]{:S(2)}) async-start(), calls=%async_computation.1 | async-start | bytes 3440640 | tf_op jit(solution)/shard_map/reduce_scatter | solution.py:693
  156.7 31.6 %collective-permute-start.5 = (bf16[672,512]{1,0:T(8,128)(2,1)}, bf16[672,512]{1,0:T(8,128)(2,1)}, u32[]{:S(2)}, u32[]{:S(2)}) collective-permute-start(bf16[672,512]{1,0:T(8,128)(2,1)} %collective-permute-done.4.refs_6_), channel_id=1, source_target_pairs={{0,16},{16,0},{1,17},{17,1},{2,18},{18,2},{3,19},{19,3},{4,20},{20... | collective-permute-start | bytes 2064392 | tf_op jit(solution)/shard_map/ppermute | solution.py:589
  173.4 12.0 %copy-start.10 = (bf16[672,512]{1,0:T(8,128)(2,1)}, bf16[672,512]{1,0:T(8,128)(2,1)S(1)}, u32[]{:S(2)}) copy-start(bf16[672,512]{1,0:T(8,128)(2,1)S(1)} %collective-permute-done.3.refs_5_) | copy-start | bytes 2064388
  173.4 29.6 %collective-permute-start.15 = (bf16[336,1024]{1,0:T(8,128)(2,1)}, bf16[336,1024]{1,0:T(8,128)(2,1)}, u32[]{:S(2)}, u32[]{:S(2)}) collective-permute-start(bf16[336,1024]{1,0:T(8,128)(2,1)} %collective-permute-done.14.refs_2_), channel_id=1, source_target_pairs={{0,16},{16,0},{1,17},{17,1},{2,18},{18,2},{3,19},{19,3},{4,20},{20... | collective-permute-start | bytes 2064392 | tf_op jit(solution)/shard_map/ppermute | solution.py:602
  174.1 42.7 %collective-permute-start.17 = (bf16[336,1024]{1,0:T(8,128)(2,1)}, bf16[336,1024]{1,0:T(8,128)(2,1)}, u32[]{:S(2)}, u32[]{:S(2)}) collective-permute-start(bf16[336,1024]{1,0:T(8,128)(2,1)} %collective-permute-done.16.refs_4_), channel_id=1, source_target_pairs={{0,16},{16,0},{1,17},{17,1},{2,18},{18,2},{3,19},{19,3},{4,20},{20... | collective-permute-start | bytes 2064392 | tf_op jit(solution)/shard_map/ppermute | solution.py:602
  188.2 28.6 %collective-permute-start.11 = (bf16[512,512]{1,0:T(8,128)(2,1)}, bf16[512,512]{1,0:T(8,128)(2,1)S(1)}, u32[]{:S(2)}, u32[]{:S(2)}) collective-permute-start(bf16[512,512]{1,0:T(8,128)(2,1)} %project.5.k0.v0), channel_id=1, source_target_pairs={{0,8},{4,12},{8,0},{12,4},{1,9},{5,13},{9,1},{13,5},{2,10},{6,14},... | collective-permute-start | bytes 1572872 | tf_op jit(solution)/shard_map/ppermute | solution.py:679
  190.0 48.1 %collective-permute-start.18 = (bf16[336,1024]{1,0:T(8,128)(2,1)}, bf16[336,1024]{1,0:T(8,128)(2,1)}, u32[]{:S(2)}, u32[]{:S(2)}) collective-permute-start(bf16[336,1024]{1,0:T(8,128)(2,1)} %collective-permute-done.14.refs_2_), channel_id=1, source_target_pairs={{0,4},{4,0},{8,12},{12,8},{1,5},{5,1},{9,13},{13,9},{2,6},{6,2},{1... | collective-permute-start | bytes 2064392 | tf_op jit(solution)/shard_map/ppermute | solution.py:604
  203.0 35.3 %collective-permute-start.20 = (bf16[336,1024]{1,0:T(8,128)(2,1)}, bf16[336,1024]{1,0:T(8,128)(2,1)}, u32[]{:S(2)}, u32[]{:S(2)}) collective-permute-start(bf16[336,1024]{1,0:T(8,128)(2,1)} %collective-permute-done.16.refs_4_), channel_id=1, source_target_pairs={{0,4},{4,0},{8,12},{12,8},{1,5},{5,1},{9,13},{13,9},{2,6},{6,2},{1... | collective-permute-start | bytes 2064392 | tf_op jit(solution)/shard_map/ppermute | solution.py:604
  216.8 21.4 %collective-permute-start.19 = (bf16[336,1024]{1,0:T(8,128)(2,1)}, bf16[336,1024]{1,0:T(8,128)(2,1)}, u32[]{:S(2)}, u32[]{:S(2)}) collective-permute-start(bf16[336,1024]{1,0:T(8,128)(2,1)} %collective-permute-done.15.refs_3_), channel_id=1, source_target_pairs={{0,4},{4,0},{8,12},{12,8},{1,5},{5,1},{9,13},{13,9},{2,6},{6,2},{1... | collective-permute-start | bytes 2064392 | tf_op jit(solution)/shard_map/ppermute | solution.py:604
  216.8 9.2 %copy-start.2 = (bf16[512,512]{1,0:T(8,128)(2,1)}, bf16[512,512]{1,0:T(8,128)(2,1)S(1)}, u32[]{:S(2)}) copy-start(bf16[512,512]{1,0:T(8,128)(2,1)S(1)} %collective-permute-done.11.k2.v2) | copy-start | bytes 1572868
  216.8 21.4 %collective-permute-start.21 = (bf16[336,1024]{1,0:T(8,128)(2,1)}, bf16[336,1024]{1,0:T(8,128)(2,1)}, u32[]{:S(2)}, u32[]{:S(2)}) collective-permute-start(bf16[336,1024]{1,0:T(8,128)(2,1)} %collective-permute-done.17.refs_5_), channel_id=1, source_target_pairs={{0,4},{4,0},{8,12},{12,8},{1,5},{5,1},{9,13},{13,9},{2,6},{6,2},{1... | collective-permute-start | bytes 2064392 | tf_op jit(solution)/shard_map/ppermute | solution.py:604
  238.0 1.5 collective-permute-start.12
  239.6 0.7 copy-start.14
  254.2 3.4 collective-permute-start.24
  257.6 1.1 copy-start.5
  279.3 1.3 collective-permute-start.25
  280.7 0.7 copy-start.15
  290.8 33.1 %copy-start.3 = (bf16[4,1344,128]{2,1,0:T(8,128)(2,1)S(1)}, bf16[4,1344,128]{2,1,0:T(8,128)(2,1)}, u32[]{:S(2)}) copy-start(bf16[4,1344,128]{2,1,0:T(8,128)(2,1)} %project_out.3) | copy-start | bytes 4128772
  293.0 45.6 %copy-start.6 = (bf16[1344,128]{1,0:T(8,128)(2,1)S(1)}, bf16[1344,128]{1,0:T(8,128)(2,1)}, u32[]{:S(2)}) copy-start(bf16[1344,128]{1,0:T(8,128)(2,1)} %multiply_convert_fusion) | copy-start | bytes 1032196
  293.0 17.8 %collective-permute-start.26 = (bf16[1344,128]{1,0:T(8,128)(2,1)}, bf16[1344,128]{1,0:T(8,128)(2,1)S(1)}, u32[]{:S(2)}, u32[]{:S(2)}) collective-permute-start(bf16[1344,128]{1,0:T(8,128)(2,1)} %get-tuple-element.16), channel_id=1, source_target_pairs={{0,1},{1,2},{2,3},{3,0},{4,5},{5,6},{6,7},{7,4},{8,9},{9,10},{10,1... | collective-permute-start | bytes 1032200 | tf_op jit(solution)/shard_map/ppermute | solution.py:560
  293.0 31.0 %collective-permute-start.27 = (bf16[1344,128]{1,0:T(8,128)(2,1)S(1)}, bf16[1344,128]{1,0:T(8,128)(2,1)S(1)}, u32[]{:S(2)}, u32[]{:S(2)}) collective-permute-start(bf16[1344,128]{1,0:T(8,128)(2,1)S(1)} %get-tuple-element.18), channel_id=1, source_target_pairs={{0,2},{1,3},{2,0},{3,1},{4,6},{5,7},{6,4},{7,5},{8,10},{9,11},{10,... | collective-permute-start | bytes 1032200 | tf_op jit(solution)/shard_map/ppermute | solution.py:560
  294.5 29.4 %collective-permute-start.28 = (bf16[1344,128]{1,0:T(8,128)(2,1)S(1)}, bf16[1344,128]{1,0:T(8,128)(2,1)S(1)}, u32[]{:S(2)}, u32[]{:S(2)}) collective-permute-start(bf16[1344,128]{1,0:T(8,128)(2,1)S(1)} %get-tuple-element.17), channel_id=1, source_target_pairs={{0,3},{1,0},{2,1},{3,2},{4,7},{5,4},{6,5},{7,6},{8,11},{9,8},{10,9... | collective-permute-start | bytes 1032200 | tf_op jit(solution)/shard_map/ppermute | solution.py:560
  323.9 14.6 %copy-start.11 = (bf16[1344,128]{1,0:T(8,128)(2,1)}, bf16[1344,128]{1,0:T(8,128)(2,1)S(1)}, u32[]{:S(2)}) copy-start(bf16[1344,128]{1,0:T(8,128)(2,1)S(1)} %collective-permute-done.27) | copy-start | bytes 1032196
  324.0 14.6 %copy-start.12 = (bf16[1344,128]{1,0:T(8,128)(2,1)}, bf16[1344,128]{1,0:T(8,128)(2,1)S(1)}, u32[]{:S(2)}) copy-start(bf16[1344,128]{1,0:T(8,128)(2,1)S(1)} %collective-permute-done.28) | copy-start | bytes 1032196
  325.5 11.2 %collective-permute-start.29 = (f32[1,384]{1,0:T(1,128)S(1)}, f32[1,384]{1,0:T(1,128)S(1)}, u32[]{:S(2)}, u32[]{:S(2)}) collective-permute-start(f32[1,384]{1,0:T(1,128)S(1)} %pad_maximum_fusion), channel_id=1, source_target_pairs={{0,1},{1,2},{2,3},{3,0},{4,5},{5,6},{6,7},{7,4},{8,9},{9,10},{10,1... | collective-permute-start | bytes 4616 | tf_op jit(solution)/shard_map/ppermute | solution.py:571
  333.5 4.5 %collective-permute-start.30 = (f32[1,384]{1,0:T(1,128)S(1)}, f32[1,384]{1,0:T(1,128)S(1)}, u32[]{:S(2)}, u32[]{:S(2)}) collective-permute-start(f32[1,384]{1,0:T(1,128)S(1)} %pad_maximum_fusion), channel_id=1, source_target_pairs={{0,2},{1,3},{2,0},{3,1},{4,6},{5,7},{6,4},{7,5},{8,10},{9,11},{10,... | collective-permute-start | bytes 4616 | tf_op jit(solution)/shard_map/ppermute | solution.py:571
  335.0 3.6 %collective-permute-start.31 = (f32[1,384]{1,0:T(1,128)S(1)}, f32[1,384]{1,0:T(1,128)S(1)}, u32[]{:S(2)}, u32[]{:S(2)}) collective-permute-start(f32[1,384]{1,0:T(1,128)S(1)} %pad_maximum_fusion), channel_id=1, source_target_pairs={{0,3},{1,0},{2,1},{3,2},{4,7},{5,4},{6,5},{7,6},{8,11},{9,8},{10,9... | collective-permute-start | bytes 4616 | tf_op jit(solution)/shard_map/ppermute | solution.py:571
  338.6 4.1 %copy-start.7 = (bf16[256,1344]{0,1:T(8,128)(2,1)S(1)}, bf16[256,1344]{0,1:T(8,128)(2,1)}, u32[]{:S(2)}) copy-start(bf16[256,1344]{0,1:T(8,128)(2,1)} %param.10) | copy-start | bytes 2064388
  338.6 4.1 %copy-start.8 = (bf16[1,1344,256]{2,1,0:T(8,128)(2,1)S(1)}, bf16[1,1344,256]{2,1,0:T(8,128)(2,1)}, u32[]{:S(2)}) copy-start(bf16[1,1344,256]{2,1,0:T(8,128)(2,1)} %reduce-scatter.2.cloned.1.call-done) | copy-start | bytes 2064388
Sparse Core Ops, SparseCore 0:
  9.5 59.6 all-gather.4
  156.6 32.4 all-gather.6
  250.5 62.0 reduce-scatter.1
